TPU v7x, 128 devices: a whole 4x4x4 slice. The times are simulated.
128 devices in a mesh: ctx: 32 (over y, x_lo, z), tp: 4 (over x_hi, core).
Axes of the slice: x: 4 (x_hi: 2, x_lo: 2; x = x_hi * 2 + x_lo), y: 4, z: 4, core: 2. Of those that a mesh axis runs over, the one named last changes fastest.
Arguments:
- query_one: bfloat16 [8192, 8192], P('ctx', 'tp'), may hold values from -6 to 6
- key_one: bfloat16 [8192, 8192], P('ctx', 'tp'), may hold values from -6 to 6
- value_one: bfloat16 [8192, 8192], P('ctx', 'tp'), may hold values from -6 to 6
- residual_in: bfloat16 [8192, 8192], P('ctx', 'tp'), may hold values from -50 to 50
- medium_taps: bfloat16 [128, 8192], P(None, 'tp'), may hold values from -0.5 to 0.5
- skip_one: float32 [8192], P('tp'), may hold values from -4 to 4
- norm_gain: float32 [8192], P('tp'), may hold values from 0.5 to 1.5
- query_two: bfloat16 [8192, 8192], P('ctx', 'tp'), may hold values from -6 to 6
- key_two: bfloat16 [8192, 8192], P('ctx', 'tp'), may hold values from -6 to 6
- residues: float32 [16, 8192], P(None, 'tp'), may hold values from -2 to 2
- decay_rates: float32 [16, 8192], P(None, 'tp'), may hold values from 0.00012207031 to 0.03
- skip_two: float32 [8192], P('tp'), may hold values from -4 to 4
Outputs:
- residual_out: bfloat16 [8192, 8192], P('ctx', 'tp')
- long_output: bfloat16 [8192, 8192], P('ctx', 'tp')
All inputs are finite; a program needn't handle non-finite values.
Results may differ from a plain program's by a relative error of at most 0.013.
Values may be sent and summed in bfloat16 or wider, within the bound.
No kernel may reach another device: no remote copies, remote signals or barrier semaphores. Data moves between devices by JAX's collectives and lax.ppermute only.
A program may use at most 128 MiB of HBM per device.

v0:
```python
import functools
import math

import jax
import jax.numpy as jnp
import numpy as np
from jax import lax
from jax.experimental import pallas as pl
from jax.experimental.pallas import tpu as pltpu
from jax.sharding import PartitionSpec as P

HALF = 128
LANES = 128
SUB = 8
STEPS = HALF // SUB
WIDE = 256


def split_table(table):
    upper = table.astype(jnp.bfloat16)
    lower = (table - upper.astype(np.float64)).astype(jnp.bfloat16)
    return upper, lower


def transform_tables(count):
    half = count // 2
    freq = np.arange(half)[:, None]
    time = np.arange(count)[None, :]
    angle = 2.0 * math.pi * ((freq * time) % count) / count
    even = np.cos(angle)
    odd = -np.sin(angle)
    odd[0] = np.where(np.arange(count) % 2 == 0, 1.0, -1.0)
    forward = np.concatenate([even, odd], axis=0)
    weight = np.full((half, 1), 2.0 / count)
    weight[0] = 1.0 / count
    backward = np.concatenate([even * weight, odd * weight], axis=0).T[half:]
    return forward, backward


def dot32(left, right):
    return jnp.dot(left, right, preferred_element_type=jnp.float32)


def on_chip(value):
    return pltpu.with_memory_space_constraint(value, pltpu.VMEM)


def local_call(kernel, name, out_shape, operands, scratch=()):
    call = pl.pallas_call(
        kernel,
        in_specs=[pl.BlockSpec(memory_space=pltpu.VMEM)] * len(operands),
        out_specs=jax.tree.map(lambda _: pl.BlockSpec(memory_space=pltpu.VMEM), out_shape),
        out_shape=jax.tree.map(lambda s: pltpu.VMEM(s.shape, s.dtype), out_shape),
        scratch_shapes=list(scratch),
        compiler_params=pltpu.CompilerParams(vmem_limit_bytes=8 << 20),
        name=name,
    )
    return call(*[on_chip(operand) for operand in operands])


def shape_of(shape, dtype):
    return jax.ShapeDtypeStruct(shape, dtype)


def tap_kernel(taps_ref, fwd_ref, even_ref, cross_ref, last_ref):
    count = 2 * HALF
    for start in range(0, taps_ref.shape[1], WIDE):
        cols = pl.ds(start, WIDE)
        both = dot32(fwd_ref[:, :HALF], taps_ref[:, cols])
        spec = both[:count] + both[count:]
        even, odd = spec[:HALF], spec[HALF:]
        first = lax.broadcasted_iota(jnp.int32, even.shape, 0) == 0
        even_ref[:, cols] = even
        cross_ref[:, cols] = jnp.where(first, 0.0, odd)
        last_ref[:, cols] = jnp.where(first, odd, even)


def filter_kernel(
    row_start,
    before_ref,
    here_ref,
    even_ref,
    cross_ref,
    last_ref,
    query_ref,
    resid_ref,
    skip_ref,
    fwd_ref,
    bwd_ref,
    out_ref,
    square_ref,
):
    count = 2 * HALF
    rows = pl.ds(row_start, HALF)
    total = None
    ahead = None
    starts = list(range(0, here_ref.shape[1], WIDE))
    for index in range(len(starts) + 1):
        spec = ahead
        if index < len(starts):
            cols = pl.ds(starts[index], WIDE)
            signal = jnp.concatenate([before_ref[:, cols], here_ref[:, cols]], axis=0)
            both = dot32(fwd_ref[...], signal)
            ahead = both[:count] + both[count:]
        if index == 0:
            continue
        cols = pl.ds(starts[index - 1], WIDE)
        sig_even, sig_odd = spec[:HALF], spec[HALF:]
        tap_cross = cross_ref[:, cols]
        joint = jnp.concatenate(
            [
                sig_even * even_ref[:, cols] - sig_odd * tap_cross,
                sig_even * tap_cross + sig_odd * last_ref[:, cols],
            ],
            axis=0,
        )
        joint_hi = joint.astype(jnp.bfloat16)
        joint_lo = (joint - joint_hi.astype(jnp.float32)).astype(jnp.bfloat16)
        back = dot32(bwd_ref[...], joint_hi)
        filtered = back[:HALF] + back[HALF:] + dot32(bwd_ref[:HALF], joint_lo)
        mixed = filtered + skip_ref[:, cols] * here_ref[:, cols].astype(jnp.float32)
        result = (
            resid_ref[rows, cols].astype(jnp.float32)
            + query_ref[rows, cols].astype(jnp.float32) * mixed
        ).astype(jnp.bfloat16)
        out_ref[:, cols] = result
        wide = result.astype(jnp.float32)
        squares = wide * wide
        for lane in range(0, WIDE, LANES):
            part = squares[:, lane : lane + LANES]
            total = part if total is None else total + part
    summed = jnp.sum(total.T, axis=0, keepdims=True)
    square_ref[...] = jnp.broadcast_to(summed, square_ref.shape)


def medium_block(before, here, spectrum, query, resid, skip, tables, row_start):
    return local_call(
        functools.partial(filter_kernel, row_start),
        "medium",
        [
            shape_of(here.shape, jnp.bfloat16),
            shape_of((SUB, HALF), jnp.float32),
        ],
        (before, here, *spectrum, query, resid, skip, *tables),
    )


def sublane_iota():
    return lax.broadcasted_iota(jnp.int32, (SUB, LANES), 0)


def row_of(ref, row, cols):
    return jnp.broadcast_to(ref[row : row + 1, cols], (SUB, LANES))


def lane_blocks(channels, body):
    def step(block, carry):
        body(block, pl.ds(pl.multiple_of(block * LANES, LANES), LANES))
        return carry

    lax.fori_loop(0, channels // LANES, step, 0)


def state_kernel(
    row_start,
    total_channels,
    with_later,
    *refs,
):
    part_ref, key_ref, near_ref, far_ref, gain_ref, rate_ref = refs[:6]
    later_ref = refs[6] if with_later else None
    value_ref, end_ref, state_ref = refs[6 + with_later : 9 + with_later]
    wide_ref, scale_ref = refs[9 + with_later :]
    modes = rate_ref.shape[0]
    blocks = end_ref.shape[0]
    rows = pl.ds(row_start, HALF)
    scale = lax.rsqrt((near_ref[...] + far_ref[...]) / total_channels + 1e-05)
    scale_ref[...] = jnp.broadcast_to(scale[:1], (HALF, HALF)).T

    def body(block, cols):
        value = (
            key_ref[rows, cols].astype(jnp.float32)
            * part_ref[:, cols].astype(jnp.float32)
            * scale_ref[...]
            * gain_ref[:, cols]
        ).astype(jnp.bfloat16)
        value_ref[:, cols] = value
        wide_ref[...] = value.astype(jnp.float32)
        rates = [row_of(rate_ref, m, cols) for m in range(modes)]
        decay = [jnp.exp(-rate) for rate in rates]
        held = [None] * modes
        for i in range(STEPS):
            step = wide_ref[pl.ds(i, SUB, stride=STEPS), :]
            for m in range(modes):
                held[m] = step if i == 0 else held[m] * decay[m] + step
        remaining = (sublane_iota() - (SUB - 1)).astype(jnp.float32) * float(STEPS)
        for m in range(modes):
            end_ref[block, m] = held[m]
            state = jnp.sum(held[m] * jnp.exp(rates[m] * remaining), axis=0, keepdims=True)
            if with_later:
                state = (
                    later_ref[m // SUB, block, m % SUB : m % SUB + 1, :]
                    + jnp.exp(-rates[m][:1] * float(HALF)) * state
                )
            state_ref[m // SUB, block, m % SUB : m % SUB + 1, :] = state

    lane_blocks(blocks * LANES, body)


def half_states(part, key, near, far, gain, rates, row_start, total_channels, later=None):
    channels = part.shape[1]
    modes = rates.shape[0]
    blocks = channels // LANES
    extra = () if later is None else (later,)
    return local_call(
        functools.partial(state_kernel, row_start, total_channels, len(extra)),
        "states",
        [
            shape_of(part.shape, jnp.bfloat16),
            shape_of((blocks, modes, SUB, LANES), jnp.float32),
            shape_of((modes // SUB, blocks, SUB, LANES), jnp.float32),
        ],
        (part, key, near, far, gain, rates, *extra),
        [pltpu.VMEM((HALF, LANES), jnp.float32), pltpu.VMEM((HALF, HALF), jnp.float32)],
    )


def scan_kernel(span, rate_ref, end_ref, start_ref):
    decay = jnp.exp(-rate_ref[...] * span)
    held = jnp.zeros_like(decay)
    for source in range(end_ref.shape[0]):
        start_ref[source] = held
        held = held * decay + end_ref[source]


def scanned(rate_tile, ends, span):
    return local_call(
        functools.partial(scan_kernel, float(span)),
        "scan",
        shape_of(ends.shape, ends.dtype),
        (rate_tile, ends),
    )


def short_kernel(low_ref, high_ref, rate_ref, residue_ref, near_ref, wide_ref, tap_ref):
    modes = rate_ref.shape[0]

    def body(block, cols):
        for start in range(0, STEPS, SUB):
            offset = (sublane_iota() + start).astype(jnp.float32)
            taps = None
            for m in range(modes):
                rate = row_of(rate_ref, m, cols)
                term = row_of(residue_ref, m, cols) * jnp.sqrt(rate) * jnp.exp(-rate * offset)
                taps = term if taps is None else taps + term
            tap_ref[start : start + SUB, :] = taps
        for half, value_ref in enumerate((low_ref, high_ref)):
            wide_ref[...] = value_ref[:, cols].astype(jnp.float32)
            steps = [wide_ref[pl.ds(i, SUB, stride=STEPS), :] for i in range(STEPS)]
            sums = [None] * STEPS
            for k in range(STEPS):
                tap = jnp.broadcast_to(tap_ref[k : k + 1, :], (SUB, LANES))
                for i in range(k, STEPS):
                    term = tap * steps[i - k]
                    sums[i] = term if k == 0 else sums[i] + term
            for i in range(STEPS):
                near_ref[half * STEPS + i, :, cols] = sums[i]

    lane_blocks(low_ref.shape[1], body)


def short_part(low, high, rates, residues):
    channels = low.shape[1]
    return local_call(
        short_kernel,
        "short",
        shape_of((2 * STEPS, SUB, channels), jnp.float32),
        (low, high, rates, residues),
        [pltpu.VMEM((HALF, LANES), jnp.float32), pltpu.VMEM((STEPS, LANES), jnp.float32)],
    )


def shifted_down(value, count):
    return jnp.where(sublane_iota() >= count, pltpu.roll(value, count, axis=0), 0.0)


def prefix_kernel(low_ref, high_ref, rate_ref, low_out_ref, high_out_ref):
    modes = rate_ref.shape[0]

    def body(block, cols):
        for m in range(modes):
            rate = row_of(rate_ref, m, cols)
            spans = [jnp.exp(rate * float(-STEPS * span)) for span in (1, 2, 4)]
            run = low_ref[block, m]
            for span, factor in zip((1, 2, 4), spans):
                run = run + factor * shifted_down(run, span)
            low_out_ref[block, m] = shifted_down(run, 1)
            carried = jnp.broadcast_to(run[SUB - 1 :], (SUB, LANES))
            run = high_ref[block, m]
            for span, factor in zip((1, 2, 4), spans):
                run = run + factor * shifted_down(run, span)
            position = sublane_iota().astype(jnp.float32) * float(-STEPS)
            high_out_ref[block, m] = shifted_down(run, 1) + jnp.exp(rate * position) * carried

    lane_blocks(low_ref.shape[0] * LANES, body)


def prefixes(low, high, rates):
    return local_call(
        prefix_kernel,
        "prefix",
        [shape_of(low.shape, low.dtype), shape_of(high.shape, high.dtype)],
        (low, high, rates),
    )


def output_kernel(
    low_ref,
    high_ref,
    near_ref,
    start_ref,
    low_prefix_ref,
    high_prefix_ref,
    rate_ref,
    residue_ref,
    query_ref,
    skip_ref,
    out_ref,
    mixed_ref,
):
    modes = rate_ref.shape[0]

    def body(block, cols):
        position = sublane_iota().astype(jnp.float32) * float(-STEPS) - 1.0
        for half, (value_ref, prefix_ref) in enumerate(
            ((low_ref, low_prefix_ref), (high_ref, high_prefix_ref))
        ):
            decay, held = [], []
            for m in range(modes):
                rate = row_of(rate_ref, m, cols)
                factor = row_of(residue_ref, m, cols) * jnp.sqrt(rate)
                start = jnp.broadcast_to(
                    start_ref[m // SUB, block, m % SUB : m % SUB + 1, :], (SUB, LANES)
                )
                one = jnp.exp(-rate)
                decay.append(one)
                reach = jnp.exp(rate * (position - float(half * HALF)))
                held.append(factor * (prefix_ref[block, m] * one + reach * start))
            for i in range(STEPS):
                if i > 0:
                    held = [h * d for h, d in zip(held, decay)]
                terms = held + [near_ref[half * STEPS + i, :, cols]]
                while len(terms) > 1:
                    odd = terms[len(terms) // 2 * 2 :]
                    terms = [a + b for a, b in zip(terms[::2], terms[1::2])] + odd
                mixed_ref[pl.ds(i, SUB, stride=STEPS), :] = terms[0]
            rows = pl.ds(half * HALF, HALF)
            out_ref[rows, cols] = (
                query_ref[rows, cols].astype(jnp.float32)
                * (mixed_ref[...] + skip_ref[:, cols] * value_ref[:, cols].astype(jnp.float32))
            ).astype(jnp.bfloat16)

    lane_blocks(query_ref.shape[1], body)


def long_output(low, high, near, starts, low_prefix, high_prefix, rates, residues, query, skip):
    return local_call(
        output_kernel,
        "output",
        shape_of(query.shape, jnp.bfloat16),
        (low, high, near, starts, low_prefix, high_prefix, rates, residues, query, skip),
        [pltpu.VMEM((HALF, LANES), jnp.float32)],
    )


def summed_over_tp(value):
    pair = lax.ppermute(value, "tp", [(0, 1), (1, 0), (2, 3), (3, 2)])
    near = value + pair
    far = lax.ppermute(near, "tp", [(0, 2), (2, 0), (1, 3), (3, 1)])
    return near, far


def on_device(
    query_one,
    key_one,
    value_one,
    residual_in,
    medium_taps,
    skip_one,
    norm_gain,
    query_two,
    key_two,
    residues,
    decay_rates,
    skip_two,
):
    rows, channels = query_one.shape
    forward, backward = transform_tables(2 * HALF)
    tables = (
        jnp.asarray(np.concatenate(split_table(forward), axis=0)),
        jnp.asarray(np.concatenate(split_table(backward), axis=0)),
    )
    skip_row = skip_one[None, :]
    gain_row = norm_gain[None, :]
    product_high = key_one[HALF:] * value_one[HALF:]
    count = lax.axis_size("ctx")
    before = lax.ppermute(product_high, "ctx", [(d, d + 1) for d in range(count - 1)])
    product_low = key_one[:HALF] * value_one[:HALF]
    spectrum = local_call(
        tap_kernel,
        "taps",
        [shape_of(medium_taps.shape, jnp.float32)] * 3,
        (medium_taps, tables[0]),
    )
    high, square_high = medium_block(
        product_low, product_high, spectrum, query_one, residual_in, skip_row, tables, HALF
    )
    sums_high = summed_over_tp(square_high)
    low, square_low = medium_block(
        before, product_low, spectrum, query_one, residual_in, skip_row, tables, 0
    )
    sums_low = summed_over_tp(square_low)
    total_channels = channels * lax.axis_size("tp")
    value_high, end_high, state_high = half_states(
        high, key_two, *sums_high, gain_row, decay_rates, HALF, total_channels
    )
    value_low, end_low, state = half_states(
        low, key_two, *sums_low, gain_row, decay_rates, 0, total_channels, state_high
    )
    tiles = state.shape[0] * state.shape[1]
    here = lax.axis_index("ctx")
    rate_tile = lax.dynamic_slice(
        decay_rates,
        (SUB * (here // state.shape[1]), LANES * (here % state.shape[1])),
        (SUB, LANES),
    )
    gathered = lax.all_to_all(
        state.reshape(tiles, SUB, LANES), "ctx", split_axis=0, concat_axis=0, tiled=True
    )
    near = short_part(value_low, value_high, decay_rates, residues)
    starts = lax.all_to_all(
        scanned(rate_tile, gathered, rows), "ctx", split_axis=0, concat_axis=0, tiled=True
    ).reshape(state.shape)
    low_prefix, high_prefix = prefixes(end_low, end_high, decay_rates)
    residual_out = jnp.concatenate([low, high], axis=0)
    result = long_output(
        value_low,
        value_high,
        near,
        starts,
        low_prefix,
        high_prefix,
        decay_rates,
        residues,
        query_two,
        skip_two[None, :],
    )
    return (residual_out, result)


def solution(mesh):
    in_specs = (
        P("ctx", "tp"),
        P("ctx", "tp"),
        P("ctx", "tp"),
        P("ctx", "tp"),
        P(None, "tp"),
        P("tp"),
        P("tp"),
        P("ctx", "tp"),
        P("ctx", "tp"),
        P(None, "tp"),
        P(None, "tp"),
        P("tp"),
    )
    out_specs = (P("ctx", "tp"), P("ctx", "tp"))
    return jax.shard_map(
        on_device, mesh=mesh, in_specs=in_specs, out_specs=out_specs, check_vma=False
    )
```

profile of v0, /device:TPU:0, one launch (start us, length us, event | category | flops | bytes accessed | tf_op | source)
XLA Modules:
  0.0 72.3 jit_solution(14388457404094897441)
XLA Ops:
  0.6 0.0 copy-start.4
  0.6 0.0 copy-start.13
  0.7 0.0 copy-start.14
  0.7 0.0 copy-start.1
  0.7 0.0 copy-start
  0.7 0.0 copy-start.15
  0.7 1.8 %slice_multiply_fusion.1 = (bf16[128,2048]{1,0:T(8,128)(2,1)S(1)}, bf16[128,2048]{1,0:T(8,128)(2,1)S(1)}) fusion(bf16[256,2048]{1,0:T(8,128)(2,1)} %param.16, bf16[256,2048]{1,0:T(8,128)(2,1)} %param.15), kind=kLoop, calls=%fused_computation.2 | loop fusion | flops 524288 | bytes 3145728 | tf_op jit(solution)/shard_map/mul | solution.py:405
  2.5 4.0 %collective-permute-start = (bf16[128,2048]{1,0:T(8,128)(2,1)S(1)}, bf16[128,2048]{1,0:T(8,128)(2,1)S(1)}, u32[]{:S(2)}, u32[]{:S(2)}) collective-permute-start(bf16[128,2048]{1,0:T(8,128)(2,1)S(1)} %get-tuple-element.32.here_ref), channel_id=1, source_target_pairs={{0,4},{4,8},{8,12},{12,16},{16,20},{20,24},{24,28},{28,32},{32,36}... | collective-permute-start | bytes 1572872 | tf_op jit(solution)/shard_map/ppermute | solution.py:407
  6.4 0.0 copy-done.4
  6.5 0.0 copy-done.14
  6.5 0.7 taps.1
  7.2 1.9 %medium.3 = (bf16[128,2048]{1,0:T(8,128)(2,1)S(1)}, f32[8,128]{1,0:T(8,128)S(1)}) custom-call(bf16[128,2048]{1,0:T(8,128)(2,1)S(1)} %get-tuple-element.33.here_ref.before_ref, bf16[128,2048]{1,0:T(8,128)(2,1)S(1)} %get-tuple-element.32.here_ref, f32[128,2048]{1,0:T(8,128)S(1)} %get-tuple-element.17.even_ref, f32[128,2048]{1,0:T(8,128)S(1)} %get-tuple-element.18.cross_ref, ...), custom_call_target="tpu_custom_call" | custom-call | tf_op jit(solution)/shard_map/medium/pallas_call | solution.py:58
  9.1 0.0 copy-start.2
  9.1 0.0 copy-start.3
  9.1 0.0 copy-start.16
  9.1 0.1 collective-permute-start.3
  9.2 8.3 %collective-permute-done.before_ref = bf16[128,2048]{1,0:T(8,128)(2,1)S(1)} collective-permute-done((bf16[128,2048]{1,0:T(8,128)(2,1)S(1)}, bf16[128,2048]{1,0:T(8,128)(2,1)S(1)}, u32[]{:S(2)}, u32[]{:S(2)}) %collective-permute-start) | collective-permute-done | bytes 524320 | tf_op jit(solution)/shard_map/ppermute | solution.py:407
  17.6 1.9 %medium.2 = (bf16[128,2048]{1,0:T(8,128)(2,1)S(1)}, f32[8,128]{1,0:T(8,128)S(1)}) custom-call(bf16[128,2048]{1,0:T(8,128)(2,1)S(1)} %collective-permute-done.before_ref, bf16[128,2048]{1,0:T(8,128)(2,1)S(1)} %get-tuple-element.33.here_ref.before_ref, f32[128,2048]{1,0:T(8,128)S(1)} %get-tuple-element.17.even_ref, ...), custom_call_target="tpu_custom_call" | custom-call | tf_op jit(solution)/shard_map/medium/pallas_call | solution.py:58
  19.5 0.1 collective-permute-start.1
  19.6 0.0 collective-permute-done.3
  19.6 3.1 %collective-permute-start.4 = (f32[8,128]{1,0:T(8,128)S(1)}, f32[8,128]{1,0:T(8,128)S(1)}, u32[]{:S(2)}, u32[]{:S(2)}) collective-permute-start(f32[8,128]{1,0:T(8,128)S(1)} %add.18.refs_2_), channel_id=1, source_target_pairs={{0,2},{2,0},{1,3},{3,1},{4,6},{6,4},{5,7},{7,5},{8,10},{10,8},{9,1... | collective-permute-start | bytes 12296 | tf_op jit(solution)/shard_map/ppermute | solution.py:379
  22.7 0.0 collective-permute-done.1
  22.7 1.0 %collective-permute-start.2 = (f32[8,128]{1,0:T(8,128)S(1)}, f32[8,128]{1,0:T(8,128)S(1)}, u32[]{:S(2)}, u32[]{:S(2)}) collective-permute-start(f32[8,128]{1,0:T(8,128)S(1)} %add.17.refs_2_), channel_id=1, source_target_pairs={{0,2},{2,0},{1,3},{3,1},{4,6},{6,4},{5,7},{7,5},{8,10},{10,8},{9,1... | collective-permute-start | bytes 12296 | tf_op jit(solution)/shard_map/ppermute | solution.py:379
  23.8 1.0 %collective-permute-done.4.refs_3_ = f32[8,128]{1,0:T(8,128)S(1)} collective-permute-done((f32[8,128]{1,0:T(8,128)S(1)}, f32[8,128]{1,0:T(8,128)S(1)}, u32[]{:S(2)}, u32[]{:S(2)}) %collective-permute-start.4) | collective-permute-done | bytes 4128 | tf_op jit(solution)/shard_map/ppermute | solution.py:379
  24.8 0.0 copy-done.3
  24.8 2.4 %states.2 = (bf16[128,2048]{1,0:T(8,128)(2,1)S(1)}, f32[16,16,8,128]{3,2,1,0:T(8,128)S(1)}, f32[2,16,8,128]{3,2,1,0:T(8,128)S(1)}) custom-call(bf16[128,2048]{1,0:T(8,128)(2,1)S(1)} %get-tuple-element.21.refs_0_, bf16[256,2048]{1,0:T(8,128)(2,1)S(1)} %copy-done.2, f32[8,128]{1,0:T(8,128)S(1)} %add.18.refs_2_, f32[8,128]{1,0:T(8,128)S(1)} %collective-permute-done.4.refs_3_, ...), custom_call_target="tpu_custom_call" | custom-call | tf_op jit(solution)/shard_map/states/pallas_call | solution.py:58
  27.2 0.6 collective-permute-done.2.refs_3_
  27.8 3.3 %states.3 = (bf16[128,2048]{1,0:T(8,128)(2,1)S(1)}, f32[16,16,8,128]{3,2,1,0:T(8,128)S(1)}, f32[2,16,8,128]{3,2,1,0:T(8,128)}) custom-call(bf16[128,2048]{1,0:T(8,128)(2,1)S(1)} %get-tuple-element.20.refs_0_, bf16[256,2048]{1,0:T(8,128)(2,1)S(1)} %copy-done.2, f32[8,128]{1,0:T(8,128)S(1)} %add.17.refs_2_, f32[8,128]{1,0:T(8,128)S(1)} %collective-permute-done.2.refs_3_, ...), custom_call_target="tpu_custom_call" | custom-call | tf_op jit(solution)/shard_map/states/pallas_call | solution.py:58
  31.1 1.0 %copy-done.5 = f32[16,16,8,128]{3,2,1,0:T(8,128)} copy-done((f32[16,16,8,128]{3,2,1,0:T(8,128)}, f32[16,16,8,128]{3,2,1,0:T(8,128)S(1)}, u32[]{:S(2)}) %copy-start.5) | copy-done | bytes 1048600
  32.1 9.2 %all-to-all-start = ((f32[32,8,128]{2,1,0:T(8,128)}), f32[32,8,128]{2,1,0:T(8,128)S(1)}, u32[]{:S(2)}, u32[]{:S(2)}) async-start(f32[32,8,128]{2,1,0:T(8,128)} %bitcast.2), calls=%async_computation | async-start | bytes 262144 | tf_op jit(solution)/shard_map/all_to_all | solution.py:437
  41.3 8.7 %all-to-all-done.end_ref = f32[32,8,128]{2,1,0:T(8,128)S(1)} async-done(((f32[32,8,128]{2,1,0:T(8,128)}), f32[32,8,128]{2,1,0:T(8,128)S(1)}, u32[]{:S(2)}, u32[]{:S(2)}) %all-to-all-start) | async-done | bytes 131104 | tf_op jit(solution)/shard_map/all_to_all | solution.py:437
  50.0 0.7 %scan.1 = f32[32,8,128]{2,1,0:T(8,128)} custom-call(f32[8,128]{1,0:T(8,128)S(1)} %dynamic_slice.3.rate_ref, f32[32,8,128]{2,1,0:T(8,128)S(1)} %all-to-all-done.end_ref), custom_call_target="tpu_custom_call" | custom-call | tf_op jit(solution)/shard_map/scan/pallas_call | solution.py:58
  50.7 3.8 %all-to-all-start.1 = ((f32[32,8,128]{2,1,0:T(8,128)}), f32[32,8,128]{2,1,0:T(8,128)S(1)}, u32[]{:S(2)}, u32[]{:S(2)}) async-start(f32[32,8,128]{2,1,0:T(8,128)} %scan.1), calls=%async_computation.1 | async-start | bytes 262144 | tf_op jit(solution)/shard_map/all_to_all | solution.py:441
  54.6 0.0 copy-start.6
  54.6 0.0 copy-start.12
  54.6 1.0 %pad_maximum_fusion = bf16[256,2048]{1,0:T(8,128)(2,1)} fusion(bf16[128,2048]{1,0:T(8,128)(2,1)S(1)} %get-tuple-element.21.refs_0_, bf16[128,2048]{1,0:T(8,128)(2,1)S(1)} %get-tuple-element.20.refs_0_), kind=kLoop, calls=%fused_computation | loop fusion | flops 2097152 | bytes 2097152 | tf_op jit(solution)/shard_map/concatenate | solution.py:445
  55.6 0.5 copy-done.6
  56.2 1.7 %prefix.1 = (f32[16,16,8,128]{3,2,1,0:T(8,128)S(1)}, f32[16,16,8,128]{3,2,1,0:T(8,128)S(1)}) custom-call(f32[16,16,8,128]{3,2,1,0:T(8,128)S(1)} %copy-done.6, f32[16,16,8,128]{3,2,1,0:T(8,128)S(1)} %get-tuple-element.29.high_ref, f32[16,2048]{1,0:T(8,128)S(1)} %copy-done.3), custom_call_target="tpu_custom_call" | custom-call | tf_op jit(solution)/shard_map/prefix/pallas_call | solution.py:58
  57.8 0.0 copy-start.8
  57.9 1.0 %copy-done.8 = f32[16,16,8,128]{3,2,1,0:T(8,128)} copy-done((f32[16,16,8,128]{3,2,1,0:T(8,128)}, f32[16,16,8,128]{3,2,1,0:T(8,128)S(1)}, u32[]{:S(2)}) %copy-start.8) | copy-done | bytes 1048600
  58.8 1.0 %copy-done.10 = f32[16,16,8,128]{3,2,1,0:T(8,128)} copy-done((f32[16,16,8,128]{3,2,1,0:T(8,128)}, f32[16,16,8,128]{3,2,1,0:T(8,128)S(1)}, u32[]{:S(2)}) %copy-start.10) | copy-done | bytes 1048600
  59.8 2.3 %short.1.near_ref = f32[32,8,2048]{2,1,0:T(8,128)S(1)} custom-call(bf16[128,2048]{1,0:T(8,128)(2,1)S(1)} %get-tuple-element.25.low_ref, bf16[128,2048]{1,0:T(8,128)(2,1)S(1)} %get-tuple-element.26.high_ref, f32[16,2048]{1,0:T(8,128)S(1)} %copy-done.3, f32[16,2048]{1,0:T(8,128)S(1)} %copy-done.12), custom_call_target="tpu_custom_call" | custom-call | tf_op jit(solution)/shard_map/short/pallas_call | solution.py:58
  62.1 1.2 %all-to-all-done.1 = f32[32,8,128]{2,1,0:T(8,128)S(1)} async-done(((f32[32,8,128]{2,1,0:T(8,128)}), f32[32,8,128]{2,1,0:T(8,128)S(1)}, u32[]{:S(2)}, u32[]{:S(2)}) %all-to-all-start.1) | async-done | bytes 131104 | tf_op jit(solution)/shard_map/all_to_all | solution.py:441
  63.3 1.2 %copy-done.7 = bf16[256,2048]{1,0:T(8,128)(2,1)S(1)} copy-done((bf16[256,2048]{1,0:T(8,128)(2,1)S(1)}, bf16[256,2048]{1,0:T(8,128)(2,1)}, u32[]{:S(2)}) %copy-start.7) | copy-done | bytes 1048600
  64.5 1.2 %copy-done.9 = f32[16,16,8,128]{3,2,1,0:T(8,128)S(1)} copy-done((f32[16,16,8,128]{3,2,1,0:T(8,128)S(1)}, f32[16,16,8,128]{3,2,1,0:T(8,128)}, u32[]{:S(2)}) %copy-start.9) | copy-done | bytes 1048600
  65.7 1.2 %copy-done.11 = f32[16,16,8,128]{3,2,1,0:T(8,128)S(1)} copy-done((f32[16,16,8,128]{3,2,1,0:T(8,128)S(1)}, f32[16,16,8,128]{3,2,1,0:T(8,128)}, u32[]{:S(2)}) %copy-start.11) | copy-done | bytes 1048600
  67.0 4.4 %output.1 = bf16[256,2048]{1,0:T(8,128)(2,1)S(1)} custom-call(bf16[128,2048]{1,0:T(8,128)(2,1)S(1)} %get-tuple-element.25.low_ref, bf16[128,2048]{1,0:T(8,128)(2,1)S(1)} %get-tuple-element.26.high_ref, f32[32,8,2048]{2,1,0:T(8,128)S(1)} %short.1.near_ref, f32[2,16,8,128]{3,2,1,0:T(8,128)S(1)} %bitcast.5, f32[16,16,8,128]{3,2,1,0:T(8,128)S(1)} %copy-done.9, ...), custom_call_target="tpu_custom_call" | custom-call | tf_op jit(solution)/shard_map/output/pallas_call | solution.py:58
  71.4 1.0 %copy.16 = bf16[256,2048]{1,0:T(8,128)(2,1)} copy(bf16[256,2048]{1,0:T(8,128)(2,1)S(1)} %output.1) | data formatting | bytes 2097152
  (17 shorter events, 0.0 us)
Async XLA Ops:
  0.6 5.8 %copy-start.4 = (bf16[512,256]{1,0:T(8,128)(2,1)S(1)}, bf16[512,256]{1,0:T(8,128)(2,1)}, u32[]{:S(2)}) copy-start(bf16[512,256]{1,0:T(8,128)(2,1)} %constant.43.clone.fwd_ref) | copy-start | bytes 786436
  0.6 6.5 %copy-start.13 = (bf16[256,256]{1,0:T(8,128)(2,1)S(1)}, bf16[256,256]{1,0:T(8,128)(2,1)}, u32[]{:S(2)}) copy-start(bf16[256,256]{1,0:T(8,128)(2,1)} %constant.44.clone.bwd_ref) | copy-start | bytes 393220
  0.7 5.8 %copy-start.14 = (bf16[128,2048]{1,0:T(8,128)(2,1)S(1)}, bf16[128,2048]{1,0:T(8,128)(2,1)}, u32[]{:S(2)}) copy-start(bf16[128,2048]{1,0:T(8,128)(2,1)} %taps_ref.1) | copy-start | bytes 1572868
  0.7 6.5 %copy-start.1 = (bf16[256,2048]{1,0:T(8,128)(2,1)S(1)}, bf16[256,2048]{1,0:T(8,128)(2,1)}, u32[]{:S(2)}) copy-start(bf16[256,2048]{1,0:T(8,128)(2,1)} %resid_ref.3) | copy-start | bytes 3145732
  0.7 6.5 %copy-start = (bf16[256,2048]{1,0:T(8,128)(2,1)S(1)}, bf16[256,2048]{1,0:T(8,128)(2,1)}, u32[]{:S(2)}) copy-start(bf16[256,2048]{1,0:T(8,128)(2,1)} %query_ref.4) | copy-start | bytes 3145732
  0.7 6.5 %copy-start.15 = (f32[2048]{0:T(1024)S(1)}, f32[2048]{0:T(1024)}, u32[]{:S(2)}) copy-start(f32[2048]{0:T(1024)} %param.19) | copy-start | bytes 24580
  2.5 15.1 %collective-permute-start = (bf16[128,2048]{1,0:T(8,128)(2,1)S(1)}, bf16[128,2048]{1,0:T(8,128)(2,1)S(1)}, u32[]{:S(2)}, u32[]{:S(2)}) collective-permute-start(bf16[128,2048]{1,0:T(8,128)(2,1)S(1)} %get-tuple-element.32.here_ref), channel_id=1, source_target_pairs={{0,4},{4,8},{8,12},{12,16},{16,20},{20,24},{24,28},{28,32},{32,36}... | collective-permute-start | bytes 1572872 | tf_op jit(solution)/shard_map/ppermute | solution.py:407
  9.1 15.7 %copy-start.2 = (bf16[256,2048]{1,0:T(8,128)(2,1)S(1)}, bf16[256,2048]{1,0:T(8,128)(2,1)}, u32[]{:S(2)}) copy-start(bf16[256,2048]{1,0:T(8,128)(2,1)} %refs_1_.3) | copy-start | bytes 3145732
  9.1 15.7 %copy-start.3 = (f32[16,2048]{1,0:T(8,128)S(1)}, f32[16,2048]{1,0:T(8,128)}, u32[]{:S(2)}) copy-start(f32[16,2048]{1,0:T(8,128)} %rate_ref.5) | copy-start | bytes 393220
  9.1 15.7 %copy-start.16 = (f32[2048]{0:T(1024)S(1)}, f32[2048]{0:T(1024)}, u32[]{:S(2)}) copy-start(f32[2048]{0:T(1024)} %param.20) | copy-start | bytes 24580
  9.1 10.4 %collective-permute-start.3 = (f32[8,128]{1,0:T(8,128)S(1)}, f32[8,128]{1,0:T(8,128)S(1)}, u32[]{:S(2)}, u32[]{:S(2)}) collective-permute-start(f32[8,128]{1,0:T(8,128)S(1)} %get-tuple-element.23), channel_id=1, source_target_pairs={{0,1},{1,0},{2,3},{3,2},{4,5},{5,4},{6,7},{7,6},{8,9},{9,8},{10,11... | collective-permute-start | bytes 12296 | tf_op jit(solution)/shard_map/ppermute | solution.py:377
  19.5 3.2 %collective-permute-start.1 = (f32[8,128]{1,0:T(8,128)S(1)}, f32[8,128]{1,0:T(8,128)S(1)}, u32[]{:S(2)}, u32[]{:S(2)}) collective-permute-start(f32[8,128]{1,0:T(8,128)S(1)} %get-tuple-element.22), channel_id=1, source_target_pairs={{0,1},{1,0},{2,3},{3,2},{4,5},{5,4},{6,7},{7,6},{8,9},{9,8},{10,11... | collective-permute-start | bytes 12296 | tf_op jit(solution)/shard_map/ppermute | solution.py:377
  19.6 5.2 %collective-permute-start.4 = (f32[8,128]{1,0:T(8,128)S(1)}, f32[8,128]{1,0:T(8,128)S(1)}, u32[]{:S(2)}, u32[]{:S(2)}) collective-permute-start(f32[8,128]{1,0:T(8,128)S(1)} %add.18.refs_2_), channel_id=1, source_target_pairs={{0,2},{2,0},{1,3},{3,1},{4,6},{6,4},{5,7},{7,5},{8,10},{10,8},{9,1... | collective-permute-start | bytes 12296 | tf_op jit(solution)/shard_map/ppermute | solution.py:379
  22.7 5.1 %collective-permute-start.2 = (f32[8,128]{1,0:T(8,128)S(1)}, f32[8,128]{1,0:T(8,128)S(1)}, u32[]{:S(2)}, u32[]{:S(2)}) collective-permute-start(f32[8,128]{1,0:T(8,128)S(1)} %add.17.refs_2_), channel_id=1, source_target_pairs={{0,2},{2,0},{1,3},{3,1},{4,6},{6,4},{5,7},{7,5},{8,10},{10,8},{9,1... | collective-permute-start | bytes 12296 | tf_op jit(solution)/shard_map/ppermute | solution.py:379
  31.1 1.0 %copy-start.5 = (f32[16,16,8,128]{3,2,1,0:T(8,128)}, f32[16,16,8,128]{3,2,1,0:T(8,128)S(1)}, u32[]{:S(2)}) copy-start(f32[16,16,8,128]{3,2,1,0:T(8,128)S(1)} %get-tuple-element.28.low_ref) | copy-start | bytes 3145732
  32.1 17.9 %all-to-all-start = ((f32[32,8,128]{2,1,0:T(8,128)}), f32[32,8,128]{2,1,0:T(8,128)S(1)}, u32[]{:S(2)}, u32[]{:S(2)}) async-start(f32[32,8,128]{2,1,0:T(8,128)} %bitcast.2), calls=%async_computation | async-start | bytes 262144 | tf_op jit(solution)/shard_map/all_to_all | solution.py:437
  50.7 12.6 %all-to-all-start.1 = ((f32[32,8,128]{2,1,0:T(8,128)}), f32[32,8,128]{2,1,0:T(8,128)S(1)}, u32[]{:S(2)}, u32[]{:S(2)}) async-start(f32[32,8,128]{2,1,0:T(8,128)} %scan.1), calls=%async_computation.1 | async-start | bytes 262144 | tf_op jit(solution)/shard_map/all_to_all | solution.py:441
  54.6 1.6 %copy-start.6 = (f32[16,16,8,128]{3,2,1,0:T(8,128)S(1)}, f32[16,16,8,128]{3,2,1,0:T(8,128)}, u32[]{:S(2)}) copy-start(f32[16,16,8,128]{3,2,1,0:T(8,128)} %copy-done.5) | copy-start | bytes 3145732
  54.6 5.2 %copy-start.12 = (f32[16,2048]{1,0:T(8,128)S(1)}, f32[16,2048]{1,0:T(8,128)}, u32[]{:S(2)}) copy-start(f32[16,2048]{1,0:T(8,128)} %residue_ref.3) | copy-start | bytes 393220
  57.8 1.0 %copy-start.8 = (f32[16,16,8,128]{3,2,1,0:T(8,128)}, f32[16,16,8,128]{3,2,1,0:T(8,128)S(1)}, u32[]{:S(2)}) copy-start(f32[16,16,8,128]{3,2,1,0:T(8,128)S(1)} %get-tuple-element.30.low_prefix_ref) | copy-start | bytes 3145732
  58.8 1.0 %copy-start.10 = (f32[16,16,8,128]{3,2,1,0:T(8,128)}, f32[16,16,8,128]{3,2,1,0:T(8,128)S(1)}, u32[]{:S(2)}) copy-start(f32[16,16,8,128]{3,2,1,0:T(8,128)S(1)} %get-tuple-element.31.high_prefix_ref) | copy-start | bytes 3145732
  59.8 3.5 %copy-start.17 = (f32[2048]{0:T(1024)S(1)}, f32[2048]{0:T(1024)}, u32[]{:S(2)}) copy-start(f32[2048]{0:T(1024)} %param.25) | copy-start | bytes 24580
  63.3 1.2 %copy-start.7 = (bf16[256,2048]{1,0:T(8,128)(2,1)S(1)}, bf16[256,2048]{1,0:T(8,128)(2,1)}, u32[]{:S(2)}) copy-start(bf16[256,2048]{1,0:T(8,128)(2,1)} %query_ref.5) | copy-start | bytes 3145732
  64.5 1.2 %copy-start.9 = (f32[16,16,8,128]{3,2,1,0:T(8,128)S(1)}, f32[16,16,8,128]{3,2,1,0:T(8,128)}, u32[]{:S(2)}) copy-start(f32[16,16,8,128]{3,2,1,0:T(8,128)} %copy-done.8) | copy-start | bytes 3145732
  65.7 1.2 %copy-start.11 = (f32[16,16,8,128]{3,2,1,0:T(8,128)S(1)}, f32[16,16,8,128]{3,2,1,0:T(8,128)}, u32[]{:S(2)}) copy-start(f32[16,16,8,128]{3,2,1,0:T(8,128)} %copy-done.10) | copy-start | bytes 3145732
where the time goes:
time: 72.7 us; the launch traced here: 72.3 us
  starting transfers between devices  21.3 us (29%)
  waiting for transfers between devices  19.9 us (27%)
  Pallas kernels  19.2 us (26%)
  local copies, waits for them, and re-layouts  8.17 us (11%)
  other arithmetic  2.82 us (4%)
  between operations  0.92 us (1%)
    pallas_call x9, Pallas kernels, local_call(): return call(*[on_chip(operand) for operand in operands])  19.2 us
    all_to_all x1, starting transfers between devices, on_device(): lax.all_to_all(state.reshape(tiles, SUB, LANES), 'ctx', split_axis=0, con...  9.21 us
    all_to_all x1, waiting for transfers between devices, on_device(): lax.all_to_all(state.reshape(tiles, SUB, LANES), 'ctx', split_axis=0, con...  8.67 us
    ppermute x1, waiting for transfers between devices, on_device(): lax.ppermute(product_high, 'ctx', [(d, d + 1) for d in range(count - 1)])  8.34 us
    unnamed x37, local copies, waits for them, and re-layouts  8.16 us
    ppermute x2, starting transfers between devices, summed_over_tp(): far = lax.ppermute(near, 'tp', [(0, 2), (2, 0), (1, 3), (3, 1)])  4.15 us
    ppermute x1, starting transfers between devices, on_device(): lax.ppermute(product_high, 'ctx', [(d, d + 1) for d in range(count - 1)])  3.97 us
    all_to_all x1, starting transfers between devices, on_device(): lax.all_to_all(scanned(rate_tile, gathered, rows), 'ctx', split_axis=0, c...  3.84 us
  transfers between devices with their start and end apart: 7, of which 5 were waited for; matrix products, arithmetic and copies ran while one was open for 1% of the time, Pallas kernels for 15%

commit v1 on v0

v1 whole, which is shorter than its diff:
```python
import functools
import math

import jax
import jax.numpy as jnp
import numpy as np
from jax import lax
from jax.experimental import pallas as pl
from jax.experimental.pallas import tpu as pltpu
from jax.sharding import PartitionSpec as P

HALF = 128
LANES = 128
SUB = 8
STEPS = HALF // SUB
WIDE = 256
GROUP = 8


def split_table(table):
    upper = table.astype(jnp.bfloat16)
    lower = (table - upper.astype(np.float64)).astype(jnp.bfloat16)
    return upper, lower


def transform_tables(count):
    half = count // 2
    freq = np.arange(half)[:, None]
    time = np.arange(count)[None, :]
    angle = 2.0 * math.pi * ((freq * time) % count) / count
    even = np.cos(angle)
    odd = -np.sin(angle)
    odd[0] = np.where(np.arange(count) % 2 == 0, 1.0, -1.0)
    forward = np.concatenate([even, odd], axis=0)
    weight = np.full((half, 1), 2.0 / count)
    weight[0] = 1.0 / count
    backward = np.concatenate([even * weight, odd * weight], axis=0).T[half:]
    return forward, backward


def dot32(left, right):
    return jnp.dot(left, right, preferred_element_type=jnp.float32)


HBM = pltpu.HBM


def local_call(
    kernel, name, out_shape, operands, scratch=(), far_in=(), far_out=(), aliases={}
):
    outputs = out_shape if isinstance(out_shape, list) else [out_shape]
    near = pl.BlockSpec(memory_space=pltpu.VMEM)
    far = pl.BlockSpec(memory_space=HBM)
    call = pl.pallas_call(
        kernel,
        in_specs=[far if k in far_in else near for k in range(len(operands))],
        out_specs=[far if k in far_out else near for k in range(len(outputs))],
        out_shape=[
            (HBM if k in far_out else pltpu.VMEM)(o.shape, o.dtype) for k, o in enumerate(outputs)
        ],
        scratch_shapes=list(scratch),
        compiler_params=pltpu.CompilerParams(vmem_limit_bytes=8 << 20),
        input_output_aliases=aliases,
        name=name,
    )
    results = call(
        *[
            pltpu.with_memory_space_constraint(operand, HBM if k in far_in else pltpu.VMEM)
            for k, operand in enumerate(operands)
        ]
    )
    return results if isinstance(out_shape, list) else results[0]


def shape_of(shape, dtype):
    return jax.ShapeDtypeStruct(shape, dtype)


def forward_part(fwd, signal):
    count = 2 * HALF
    both = dot32(fwd, signal)
    return both[:count] + both[count:]


def filtered_result(spec, taps, here, skip, query, resid, bwd):
    even, cross, last = taps
    sig_even, sig_odd = spec[:HALF], spec[HALF:]
    joint = jnp.concatenate(
        [sig_even * even - sig_odd * cross, sig_even * cross + sig_odd * last], axis=0
    )
    joint_hi = joint.astype(jnp.bfloat16)
    joint_lo = (joint - joint_hi.astype(jnp.float32)).astype(jnp.bfloat16)
    back = dot32(bwd, joint_hi)
    filtered = back[:HALF] + back[HALF:] + dot32(bwd[:HALF], joint_lo)
    mixed = filtered + skip * here.astype(jnp.float32)
    return (resid.astype(jnp.float32) + query.astype(jnp.float32) * mixed).astype(jnp.bfloat16)


def squares_added(total, result):
    wide = result.astype(jnp.float32)
    squares = wide * wide
    for lane in range(0, WIDE, LANES):
        part = squares[:, lane : lane + LANES]
        total = part if total is None else total + part
    return total


def write_squares(total, square_ref):
    summed = jnp.sum(total.T, axis=0, keepdims=True)
    square_ref[...] = jnp.broadcast_to(summed, square_ref.shape)


def upper_kernel(
    here_ref,
    key_far,
    value_far,
    taps_far,
    fwd_far,
    bwd_far,
    query_far,
    resid_far,
    skip_far,
    out_ref,
    square_ref,
    before_ref,
    even_ref,
    cross_ref,
    last_ref,
    key_ref,
    value_ref,
    taps_ref,
    fwd_ref,
    bwd_ref,
    query_ref,
    resid_ref,
    skip_ref,
    sems,
):
    rows = pl.ds(HALF, HALF)
    first_rows = pl.ds(0, HALF)
    copies = [
        pltpu.make_async_copy(source, target, sems.at[k])
        for k, (source, target) in enumerate(
            (
                (fwd_far, fwd_ref),
                (taps_far, taps_ref),
                (key_far.at[first_rows, :], key_ref),
                (value_far.at[first_rows, :], value_ref),
                (bwd_far, bwd_ref),
                (query_far.at[rows, :], query_ref),
                (resid_far.at[rows, :], resid_ref),
                (skip_far, skip_ref),
            )
        )
    ]
    for copy in copies:
        copy.start()
    total = None
    starts = list(range(0, here_ref.shape[1], WIDE))
    specs = {}
    for index in range(len(starts) + 2):
        if index < len(starts):
            cols = pl.ds(starts[index], WIDE)
            if index == 0:
                copies[0].wait()
                copies[1].wait()
            spec = forward_part(fwd_ref[:, :HALF], taps_ref[:, cols])
            even, odd = spec[:HALF], spec[HALF:]
            first = lax.broadcasted_iota(jnp.int32, even.shape, 0) == 0
            even_ref[:, cols] = even
            cross_ref[:, cols] = jnp.where(first, 0.0, odd)
            last_ref[:, cols] = jnp.where(first, odd, even)
        if 1 <= index <= len(starts):
            cols = pl.ds(starts[index - 1], WIDE)
            if index == 1:
                copies[2].wait()
                copies[3].wait()
            before = (
                key_ref[:, cols].astype(jnp.float32) * value_ref[:, cols].astype(jnp.float32)
            ).astype(jnp.bfloat16)
            before_ref[:, cols] = before
            signal = jnp.concatenate([before, here_ref[:, cols]], axis=0)
            specs[index - 1] = forward_part(fwd_ref[...], signal)
        if index >= 2:
            cols = pl.ds(starts[index - 2], WIDE)
            if index == 2:
                for copy in copies[4:]:
                    copy.wait()
            result = filtered_result(
                specs.pop(index - 2),
                (even_ref[:, cols], cross_ref[:, cols], last_ref[:, cols]),
                here_ref[:, cols],
                skip_ref[:, cols],
                query_ref[:, cols],
                resid_ref[:, cols],
                bwd_ref[...],
            )
            out_ref[:, cols] = result
            total = squares_added(total, result)
    write_squares(total, square_ref)


def upper_block(here, key, value, taps, tables, query, resid, skip):
    half = shape_of(here.shape, jnp.bfloat16)
    spectrum = shape_of(taps.shape, jnp.float32)
    return local_call(
        upper_kernel,
        "upper",
        [half, shape_of((SUB, HALF), jnp.float32), half, spectrum, spectrum, spectrum],
        (here, key, value, taps, *tables, query, resid, skip),
        [
            pltpu.VMEM(here.shape, jnp.bfloat16),
            pltpu.VMEM(here.shape, jnp.bfloat16),
            pltpu.VMEM(taps.shape, jnp.bfloat16),
            pltpu.VMEM(tables[0].shape, jnp.bfloat16),
            pltpu.VMEM(tables[1].shape, jnp.bfloat16),
            pltpu.VMEM(here.shape, jnp.bfloat16),
            pltpu.VMEM(here.shape, jnp.bfloat16),
            pltpu.VMEM(skip.shape, jnp.float32),
            pltpu.SemaphoreType.DMA((8,)),
        ],
        far_in=tuple(range(1, 9)),
    )


def lower_kernel(
    before_ref,
    here_ref,
    even_ref,
    cross_ref,
    last_ref,
    query_ref,
    resid_ref,
    skip_ref,
    fwd_ref,
    bwd_ref,
    out_ref,
    square_ref,
):
    rows = pl.ds(0, HALF)
    total = None
    spec = None
    starts = list(range(0, here_ref.shape[1], WIDE))
    for index in range(len(starts) + 1):
        ready = spec
        if index < len(starts):
            cols = pl.ds(starts[index], WIDE)
            signal = jnp.concatenate([before_ref[:, cols], here_ref[:, cols]], axis=0)
            spec = forward_part(fwd_ref[...], signal)
        if index > 0:
            cols = pl.ds(starts[index - 1], WIDE)
            result = filtered_result(
                ready,
                (even_ref[:, cols], cross_ref[:, cols], last_ref[:, cols]),
                here_ref[:, cols],
                skip_ref[:, cols],
                query_ref[rows, cols],
                resid_ref[rows, cols],
                bwd_ref[...],
            )
            out_ref[:, cols] = result
            total = squares_added(total, result)
    write_squares(total, square_ref)


def lower_block(before, here, spectrum, query, resid, skip, tables):
    return local_call(
        lower_kernel,
        "lower",
        [shape_of(here.shape, jnp.bfloat16), shape_of((SUB, HALF), jnp.float32)],
        (before, here, *spectrum, query, resid, skip, *tables),
    )


def sublane_iota():
    return lax.broadcasted_iota(jnp.int32, (SUB, LANES), 0)


def row_of(ref, row, cols):
    return jnp.broadcast_to(ref[row : row + 1, cols], (SUB, LANES))


def lane_blocks(channels, body):
    def step(pair, carry):
        for side in range(2):
            block = pair * 2 + side
            body(block, column(block), side)
        return carry

    lax.fori_loop(0, channels // (2 * LANES), step, 0)


def column(block):
    return pl.ds(pl.multiple_of(block * LANES, LANES), LANES)


def state_kernel(row_start, total_channels, last, *refs):
    part_ref, key_ref, near_ref, far_ref, gain_ref, rate_ref = refs[:6]
    if last:
        later_ref = refs[6]
        refs = refs[2:]
    value_ref, end_ref, state_ref, joined_ref, wide_ref, scale_ref, decay_ref, sems = refs[6:14]
    held_ref = end_ref if last else refs[14]
    join = pltpu.make_async_copy(
        part_ref, joined_ref.at[pl.ds(row_start, HALF), :], sems.at[0]
    )
    join.start()
    modes = rate_ref.shape[0]
    blocks = end_ref.shape[0]
    rows = pl.ds(row_start, HALF)
    scale = lax.rsqrt((near_ref[...] + far_ref[...]) / total_channels + 1e-05)
    scale_ref[...] = jnp.broadcast_to(scale[:1], (HALF, HALF)).T

    def body(block, cols, side):
        decay_ref[side] = jnp.exp(-rate_ref[:, cols])
        value = (
            key_ref[rows, cols].astype(jnp.float32)
            * part_ref[:, cols].astype(jnp.float32)
            * scale_ref[...]
            * gain_ref[:, cols]
        ).astype(jnp.bfloat16)
        value_ref[:, cols] = value
        wide_ref[side] = value.astype(jnp.float32)
        every = pl.ds(0, LANES)
        decay = [row_of(decay_ref.at[side], m, every) for m in range(modes)]
        held = [None] * modes
        for i in range(STEPS):
            step = wide_ref[side, pl.ds(i, SUB, stride=STEPS), :]
            for m in range(modes):
                held[m] = step if i == 0 else held[m] * decay[m] + step
        remaining = (sublane_iota() - (SUB - 1)).astype(jnp.float32) * float(STEPS)
        for m in range(modes):
            held_ref[block, m] = held[m]
        if not last:
            pltpu.make_async_copy(held_ref.at[block], end_ref.at[block], sems.at[1]).start()
        tiles = []
        for group in range(modes // SUB):
            span = range(group * SUB, (group + 1) * SUB)
            state = gathered_sums(
                [held[m] * jnp.exp(row_of(rate_ref, m, cols) * remaining) for m in span]
            )
            if last:
                rate = rate_ref[group * SUB : (group + 1) * SUB, cols]
                state = later_ref[group, block] + jnp.exp(-rate * float(HALF)) * state
            tiles.append(state)
        if last:
            joint = jnp.concatenate(tiles, axis=0).astype(jnp.bfloat16)
            for member in range(GROUP):
                state_ref[member, :, cols] = joint
        else:
            for group, state in enumerate(tiles):
                state_ref[group, block] = state

    lane_blocks(blocks * LANES, body)
    join.wait()
    if not last:
        pltpu.make_async_copy(held_ref, end_ref, sems.at[1]).wait()


def gathered_sums(values):
    row = sublane_iota()
    span = 1
    while span < SUB:
        upper = (row & span) != 0
        values = [
            jnp.where(upper, b, a) + pltpu.roll(jnp.where(upper, a, b), span, axis=0)
            for a, b in zip(values[::2], values[1::2])
        ]
        span *= 2
    return values[0]


def half_states(part, key, near, far, gain, rates, row_start, total_channels, last=()):
    channels = part.shape[1]
    modes = rates.shape[0]
    blocks = channels // LANES
    ends = (blocks, modes, SUB, LANES)
    joined = shape_of((2 * HALF, channels), jnp.bfloat16)
    scratch = [
        pltpu.VMEM((2, HALF, LANES), jnp.float32),
        pltpu.VMEM((HALF, HALF), jnp.float32),
        pltpu.VMEM((2, modes, LANES), jnp.float32),
        pltpu.SemaphoreType.DMA((2,)),
    ]
    if not last:
        scratch += [pltpu.VMEM(ends, jnp.float32)]
    return local_call(
        functools.partial(state_kernel, row_start, total_channels, len(last)),
        "states",
        [
            shape_of(part.shape, jnp.bfloat16),
            shape_of(ends, jnp.float32),
            shape_of((GROUP, modes, channels), jnp.bfloat16)
            if last
            else shape_of((modes // SUB, blocks, SUB, LANES), jnp.float32),
            joined,
        ],
        (part, key, near, far, gain, rates, *last),
        scratch,
        far_in=(7,) if last else (),
        far_out=(3,) if last else (1, 3),
        aliases={7: 3} if last else {},
    )


def member_index():
    return lax.rem(lax.axis_index("ctx"), GROUP)


def group_kernel(span, rate_ref, state_ref, total_ref, before_ref):
    member = member_index()

    def body(block, cols, side):
        decay = jnp.exp(rate_ref[:, cols] * -span)
        held = jnp.zeros_like(decay)
        before = held
        for source in range(GROUP):
            if source > 0:
                before = jnp.where(member == source, held, before)
            held = held * decay + state_ref[source, :, cols].astype(jnp.float32)
        total_ref[:, cols] = held.astype(jnp.bfloat16)
        before_ref[:, cols] = before

    lane_blocks(rate_ref.shape[1], body)


def group_scan(rates, states, span):
    return local_call(
        functools.partial(group_kernel, float(span)),
        "group",
        [shape_of(rates.shape, jnp.bfloat16), shape_of(rates.shape, jnp.float32)],
        (rates, states),
    )


def shifted_down(value, count):
    return jnp.where(sublane_iota() >= count, pltpu.roll(value, count, axis=0), 0.0)


def tree_sum(terms):
    while len(terms) > 1:
        odd = terms[len(terms) // 2 * 2 :]
        terms = [a + b for a, b in zip(terms[::2], terms[1::2])] + odd
    return terms[0]


def short_kernel(
    low_ref, high_ref, rate_ref, residue_ref, skip_ref, near_ref, wide_ref, tap_ref, made_ref, sem
):
    modes = rate_ref.shape[0]

    def body(block, cols, side):
        for start in range(0, STEPS, SUB):
            offset = (sublane_iota() + start).astype(jnp.float32)
            terms = []
            for m in range(modes):
                rate = row_of(rate_ref, m, cols)
                factor = row_of(residue_ref, m, cols) * jnp.sqrt(rate)
                terms.append(factor * jnp.exp(-rate * offset))
            tap_ref[side, start : start + SUB, :] = tree_sum(terms)
        for half, value_ref in enumerate((low_ref, high_ref)):
            wide_ref[side, half] = value_ref[:, cols].astype(jnp.float32)
            steps = [wide_ref[side, half, pl.ds(i, SUB, stride=STEPS), :] for i in range(STEPS)]
            skip = jnp.broadcast_to(skip_ref[:, cols], (SUB, LANES))
            sums = [None] * STEPS
            for k in range(STEPS):
                tap = jnp.broadcast_to(tap_ref[side, k : k + 1, :], (SUB, LANES))
                if k == 0:
                    tap = tap + skip
                for i in range(k, STEPS):
                    term = tap * steps[i - k]
                    sums[i] = term if k == 0 else sums[i] + term
            for i in range(STEPS):
                made_ref[block, pl.ds((half * STEPS + i) * SUB, SUB), :] = sums[i]
        pltpu.make_async_copy(made_ref.at[block], near_ref.at[block], sem).start()

    lane_blocks(low_ref.shape[1], body)
    pltpu.make_async_copy(made_ref, near_ref, sem).wait()


def short_part(low, high, rates, residues, skip):
    shape = (low.shape[1] // LANES, 2 * HALF, LANES)
    return local_call(
        short_kernel,
        "short",
        shape_of(shape, jnp.float32),
        (low, high, rates, residues, skip),
        [
            pltpu.VMEM((2, 2, HALF, LANES), jnp.float32),
            pltpu.VMEM((2, STEPS, LANES), jnp.float32),
            pltpu.VMEM(shape, jnp.float32),
            pltpu.SemaphoreType.DMA(()),
        ],
        far_out=(0,),
    )


def weights_of(residue_ref, rate_ref):
    rates = rate_ref[...]
    return residue_ref[...] * jnp.sqrt(rates) * jnp.exp(-rates)


def prefix_kernel(
    low_ref, far_high_ref, rate_ref, residue_ref, out_ref, weight_ref, high_ref, sems
):
    modes = rate_ref.shape[0]
    blocks = low_ref.shape[0]

    def arriving(block):
        return pltpu.make_async_copy(far_high_ref.at[block], high_ref.at[block], sems.at[block])

    for block in range(blocks):
        arriving(block).start()
    weight_ref[...] = weights_of(residue_ref, rate_ref)

    def body(block, cols, side):
        arriving(block).wait()
        for m in range(modes):
            rate = row_of(rate_ref, m, cols)
            weight = row_of(weight_ref, m, cols)
            spans = [jnp.exp(rate * float(-STEPS * span)) for span in (1, 2, 4)]
            run = low_ref[block, m]
            for span, factor in zip((1, 2, 4), spans):
                run = run + factor * shifted_down(run, span)
            out_ref[block, 0, m] = shifted_down(run, 1) * weight
            carried = jnp.broadcast_to(run[SUB - 1 :], (SUB, LANES))
            run = high_ref[block, m]
            for span, factor in zip((1, 2, 4), spans):
                run = run + factor * shifted_down(run, span)
            position = sublane_iota().astype(jnp.float32) * float(-STEPS)
            out_ref[block, 1, m] = (
                shifted_down(run, 1) + jnp.exp(rate * position) * carried
            ) * weight

    lane_blocks(blocks * LANES, body)


def prefixes(low, high, rates, residues):
    blocks, modes = low.shape[:2]
    return local_call(
        prefix_kernel,
        "prefix",
        shape_of((blocks, 2, modes, SUB, LANES), low.dtype),
        (low, high, rates, residues),
        [
            pltpu.VMEM(rates.shape, rates.dtype),
            pltpu.VMEM(high.shape, high.dtype),
            pltpu.SemaphoreType.DMA((blocks,)),
        ],
        far_in=(1,),
    )


def output_kernel(
    lag,
    near_ref,
    prefix_ref,
    before_ref,
    one_ref,
    two_ref,
    three_ref,
    rate_ref,
    residue_ref,
    query_ref,
    out_ref,
    mixed_ref,
    ready_ref,
    nears_ref,
    queries_ref,
    gain_ref,
    decay_ref,
    weight_ref,
    sems,
    out_sem,
):
    modes = rate_ref.shape[0]
    blocks = near_ref.shape[0]

    def arriving(block):
        return (
            pltpu.make_async_copy(near_ref.at[block], nears_ref.at[block], sems.at[0, block]),
            pltpu.make_async_copy(
                query_ref.at[:, column(block)], queries_ref.at[block], sems.at[1, block]
            ),
        )

    for block in range(blocks):
        for copy in arriving(block):
            copy.start()
    decay_ref[...] = jnp.exp(-rate_ref[...])
    rates = rate_ref[...]
    member = member_index().astype(jnp.float32)
    span = float(2 * HALF)
    level = jnp.exp(rates * (-span * GROUP))
    earlier = one_ref[...].astype(jnp.float32) + level * (
        two_ref[...].astype(jnp.float32) + level * three_ref[...].astype(jnp.float32)
    )
    start = before_ref[...] + jnp.exp(rates * (-span * member)) * earlier
    weight_ref[...] = weights_of(residue_ref, rate_ref) * start

    def corrected(block, side):
        cols = column(block)
        every = pl.ds(0, LANES)
        for group in range(modes // SUB):
            span = slice(group * SUB, (group + 1) * SUB)
            gain = weight_ref[span, cols]
            gain_ref[side, 0, span, :] = gain
            gain_ref[side, 1, span, :] = gain * jnp.exp(rate_ref[span, cols] * float(-HALF))
        position = sublane_iota().astype(jnp.float32) * float(-STEPS)
        decay = [row_of(decay_ref, m, cols) for m in range(modes)]
        held = [[], []]
        for m in range(modes):
            reach = jnp.exp(row_of(rate_ref, m, cols) * position)
            for half in range(2):
                gain = row_of(gain_ref.at[side, half], m, every)
                held[half].append(prefix_ref[block, half, m] + reach * gain)
        for i in range(STEPS):
            for half in range(2):
                if i > 0:
                    held[half] = [h * d for h, d in zip(held[half], decay)]
                mixed_ref[block, pl.ds((half * STEPS + i) * SUB, SUB), :] = tree_sum(held[half])

    def finished(block):
        cols = column(block)
        for copy in arriving(block):
            copy.wait()
        nears_ref[block] = nears_ref[block] + mixed_ref[block]
        for half in range(2):
            for s in range(SUB):
                rows = pl.ds(half * HALF + s * STEPS, STEPS)
                mixed = nears_ref[block, pl.ds(half * HALF + s, STEPS, stride=SUB), :]
                ready_ref[rows, cols] = (
                    queries_ref[block, rows, :].astype(jnp.float32) * mixed
                ).astype(jnp.bfloat16)
        pltpu.make_async_copy(ready_ref.at[:, cols], out_ref.at[:, cols], out_sem).start()

    for block in range(lag):
        corrected(block, block % 2)

    def step(pair, carry):
        for side in range(2):
            block = lag + pair * 2 + side
            finished(block - lag)
            corrected(block, side)
        return carry

    lax.fori_loop(0, (blocks - lag) // 2, step, 0)
    for block in range(blocks - lag, blocks):
        finished(block)
    pltpu.make_async_copy(ready_ref, out_ref, out_sem).wait()


def long_output(near, prefix, before, earlier, rates, residues, query):
    blocks = near.shape[0]
    return local_call(
        functools.partial(output_kernel, 2),
        "output",
        shape_of(query.shape, jnp.bfloat16),
        (near, prefix, before, *earlier, rates, residues, query),
        [
            pltpu.VMEM(near.shape, jnp.float32),
            pltpu.VMEM(query.shape, jnp.bfloat16),
            pltpu.VMEM(near.shape, jnp.float32),
            pltpu.VMEM((blocks, 2 * HALF, LANES), jnp.bfloat16),
            pltpu.VMEM((2, 2, *rates.shape[:1], LANES), jnp.float32),
            pltpu.VMEM(rates.shape, jnp.float32),
            pltpu.VMEM(rates.shape, jnp.float32),
            pltpu.SemaphoreType.DMA((2, blocks)),
            pltpu.SemaphoreType.DMA(()),
        ],
        far_in=(0, 8),
        far_out=(0,),
    )


def summed_with_pair(value):
    return value + lax.ppermute(value, "tp", [(0, 1), (1, 0), (2, 3), (3, 2)])


def across_pairs(value):
    return lax.ppermute(value, "tp", [(0, 2), (2, 0), (1, 3), (3, 1)])


def on_device(
    query_one,
    key_one,
    value_one,
    residual_in,
    medium_taps,
    skip_one,
    norm_gain,
    query_two,
    key_two,
    residues,
    decay_rates,
    skip_two,
):
    rows, channels = query_one.shape
    forward, backward = transform_tables(2 * HALF)
    tables = (
        jnp.asarray(np.concatenate(split_table(forward), axis=0)),
        jnp.asarray(np.concatenate(split_table(backward), axis=0)),
    )
    skip_row = skip_one[None, :]
    gain_row = norm_gain[None, :]
    skip_long = skip_two[None, :]
    product_high = key_one[HALF:] * value_one[HALF:]
    count = lax.axis_size("ctx")
    before = lax.ppermute(product_high, "ctx", [(d, d + 1) for d in range(count - 1)])
    high, square_high, product_low, *spectrum = upper_block(
        product_high, key_one, value_one, medium_taps, tables, query_one, residual_in, skip_row
    )
    near_high = summed_with_pair(square_high)
    far_high = across_pairs(near_high)
    total_channels = channels * lax.axis_size("tp")
    value_high, end_high, state_high, residual_out = half_states(
        high, key_two, near_high, far_high, gain_row, decay_rates, HALF, total_channels
    )
    before, state_high = lax.optimization_barrier((before, state_high))
    low, square_low = lower_block(
        before, product_low, spectrum, query_one, residual_in, skip_row, tables
    )
    near_low = summed_with_pair(square_low)
    far_low = across_pairs(near_low)
    value_low, end_low, state, residual_out = half_states(
        low,
        key_two,
        near_low,
        far_low,
        gain_row,
        decay_rates,
        0,
        total_channels,
        (state_high, residual_out),
    )
    members = [
        [first + k for k in range(GROUP)] for first in range(0, lax.axis_size("ctx"), GROUP)
    ]
    gathered = lax.all_to_all(
        state, "ctx", split_axis=0, concat_axis=0, tiled=True, axis_index_groups=members
    )
    near = short_part(value_low, value_high, decay_rates, residues, skip_long)
    prefix = prefixes(end_low, end_high, decay_rates, residues)
    gathered, near, prefix = lax.optimization_barrier((gathered, near, prefix))
    total, before_here = group_scan(decay_rates, gathered, rows)
    earlier = [
        lax.ppermute(total, "ctx", [(d, d + far) for d in range(count - far)])
        for far in range(GROUP, count, GROUP)
    ]
    result = long_output(
        near, prefix, before_here, earlier, decay_rates, residues, query_two
    )
    return (residual_out, result)


def solution(mesh):
    in_specs = (
        P("ctx", "tp"),
        P("ctx", "tp"),
        P("ctx", "tp"),
        P("ctx", "tp"),
        P(None, "tp"),
        P("tp"),
        P("tp"),
        P("ctx", "tp"),
        P("ctx", "tp"),
        P(None, "tp"),
        P(None, "tp"),
        P("tp"),
    )
    out_specs = (P("ctx", "tp"), P("ctx", "tp"))
    return jax.shard_map(
        on_device, mesh=mesh, in_specs=in_specs, out_specs=out_specs, check_vma=False
    )
```

time: 72.7 us -> 66.2 us (0.911)
  waiting for transfers between devices: 19.9 us -> 10.2 us
  starting transfers between devices: 21.3 us -> 27.2 us
  local copies, waits for them, and re-layouts: 8.17 us -> 3.08 us
  Pallas kernels: 19.2 us -> 22.5 us
  other arithmetic: 2.82 us -> 1.26 us
    ppermute x4 -> x7, starting transfers between devices: 4.32 us -> 15 us  [the longest x3 8.76 us: on_device(): lax.ppermute(total, 'ctx', [(d, d + far) for d in range(count - far)])]
    ppermute x1, waiting for transfers between devices: 8.34 us -> 0.01 us  [on_device(): lax.ppermute(product_high, 'ctx', [(d, d + 1) for d in range(count - 1)])]
    all_to_all x2 -> x1, waiting for transfers between devices: 9.87 us -> 1.82 us  [on_device(): lax.all_to_all(state, 'ctx', split_axis=0, concat_axis=0, tiled=True, axi...]
    ppermute x4 -> x7, waiting for transfers between devices: 1.67 us -> 8.36 us  [the longest x2 4.18 us: across_pairs(): return lax.ppermute(value, 'tp', [(0, 2), (2, 0), (1, 3), (3, 1)])]
    unnamed x37 -> x28, local copies, waits for them, and re-layouts: 8.16 us -> 3.08 us
    all_to_all x2 -> x1, starting transfers between devices: 13 us -> 8.28 us  [on_device(): lax.all_to_all(state, 'ctx', split_axis=0, concat_axis=0, tiled=True, axi...]
    pallas_call x9 -> x8, Pallas kernels: 19.2 us -> 22.5 us  [local_call(): call(*[pltpu.with_memory_space_constraint(operand, HBM if k in far_in els...]
    concatenate x1 -> x0, other arithmetic: 1.04 us -> none  [on_device(): residual_out = jnp.concatenate([low, high], axis=0)]
  transfers between devices with their start and end apart: 7 -> 9, of which waited for: 5 -> 6; matrix products, arithmetic and copies ran while one was open for 1% -> 0% of each run, Pallas kernels for 15% -> 19%
where the time goes in v1:
time: 66.2 us; the launch traced here: 65.1 us
  starting transfers between devices  27.2 us (41%)
  Pallas kernels  22.5 us (34%)
  waiting for transfers between devices  10.2 us (15%)
  local copies, waits for them, and re-layouts  3.08 us (5%)
  other arithmetic  1.26 us (2%)
  between operations  0.91 us (1%)
    pallas_call x8, Pallas kernels, local_call(): call(*[pltpu.with_memory_space_constraint(operand, HBM if k in far_in els...  22.5 us
    ppermute x3, starting transfers between devices, on_device(): lax.ppermute(total, 'ctx', [(d, d + far) for d in range(count - far)])  8.76 us
    all_to_all x1, starting transfers between devices, on_device(): lax.all_to_all(state, 'ctx', split_axis=0, concat_axis=0, tiled=True, axi...  8.28 us
    ppermute x2, starting transfers between devices, across_pairs(): return lax.ppermute(value, 'tp', [(0, 2), (2, 0), (1, 3), (3, 1)])  6.04 us
    ppermute x2, waiting for transfers between devices, across_pairs(): return lax.ppermute(value, 'tp', [(0, 2), (2, 0), (1, 3), (3, 1)])  4.18 us
    ppermute x1, starting transfers between devices, on_device(): lax.ppermute(product_high, 'ctx', [(d, d + 1) for d in range(count - 1)])  3.97 us
    unnamed x28, local copies, waits for them, and re-layouts  3.08 us
    ppermute x2, waiting for transfers between devices, summed_with_pair(): return value + lax.ppermute(value, 'tp', [(0, 1), (1, 0), (2, 3), (3, 2)])  2.31 us
  transfers between devices with their start and end apart: 9, of which 6 were waited for; matrix products, arithmetic and copies ran while one was open for 0% of the time, Pallas kernels for 19%

profile of v1, /device:TPU:0, one launch (start us, length us, event | category | flops | bytes accessed | tf_op | source)
XLA Modules:
  0.0 65.1 jit_solution(5351718051149823961)
XLA Ops:
  0.6 1.3 %slice_multiply_fusion.here_ref = bf16[128,2048]{1,0:T(8,128)(2,1)S(1)} fusion(bf16[256,2048]{1,0:T(8,128)(2,1)} %value_far.1, bf16[256,2048]{1,0:T(8,128)(2,1)} %key_far.1), kind=kLoop, calls=%fused_computation | loop fusion | flops 262144 | bytes 1572864 | tf_op jit(solution)/shard_map/mul | solution.py:707
  1.9 4.0 %collective-permute-start = (bf16[128,2048]{1,0:T(8,128)(2,1)S(1)}, bf16[128,2048]{1,0:T(8,128)(2,1)S(1)}, u32[]{:S(2)}, u32[]{:S(2)}) collective-permute-start(bf16[128,2048]{1,0:T(8,128)(2,1)S(1)} %slice_multiply_fusion.here_ref), channel_id=1, source_target_pairs={{0,4},{4,8},{8,12},{12,16},{16,20},{20,24},{24,28},{28,32},{32,36}... | collective-permute-start | bytes 1572872 | tf_op jit(solution)/shard_map/ppermute | solution.py:709
  5.9 0.0 copy-start
  5.9 0.0 copy-start.3
  5.9 0.0 copy-start.12
  5.9 0.0 copy-start.2
  5.9 0.0 copy-start.7
  5.9 0.0 copy-start.8
  5.9 0.0 copy-start.11
  5.9 3.9 %upper.1 = (bf16[128,2048]{1,0:T(8,128)(2,1)S(1)}, f32[8,128]{1,0:T(8,128)S(1)}, bf16[128,2048]{1,0:T(8,128)(2,1)S(1)}, f32[128,2048]{1,0:T(8,128)S(1)}, f32[128...) custom-call(bf16[128,2048]{1,0:T(8,128)(2,1)S(1)} %slice_multiply_fusion.here_ref, bf16[256,2048]{1,0:T(8,128)(2,1)} %key_far.1, ...), custom_call_target="tpu_custom_call" | custom-call | tf_op jit(solution)/shard_map/upper/pallas_call | solution.py:66
  9.8 0.0 copy-start.1
  9.8 0.1 collective-permute-start.1
  9.9 1.2 %collective-permute-done.1 = f32[8,128]{1,0:T(8,128)S(1)} collective-permute-done((f32[8,128]{1,0:T(8,128)S(1)}, f32[8,128]{1,0:T(8,128)S(1)}, u32[]{:S(2)}, u32[]{:S(2)}) %collective-permute-start.1) | collective-permute-done | bytes 4128 | tf_op jit(solution)/shard_map/ppermute | solution.py:677
  11.1 3.0 %collective-permute-start.2 = (f32[8,128]{1,0:T(8,128)S(1)}, f32[8,128]{1,0:T(8,128)S(1)}, u32[]{:S(2)}, u32[]{:S(2)}) collective-permute-start(f32[8,128]{1,0:T(8,128)S(1)} %add.6.refs_2_), channel_id=1, source_target_pairs={{0,2},{2,0},{1,3},{3,1},{4,6},{6,4},{5,7},{7,5},{8,10},{10,8},{9,1... | collective-permute-start | bytes 12296 | tf_op jit(solution)/shard_map/ppermute | solution.py:681
  14.1 2.1 %collective-permute-done.2.refs_3_ = f32[8,128]{1,0:T(8,128)S(1)} collective-permute-done((f32[8,128]{1,0:T(8,128)S(1)}, f32[8,128]{1,0:T(8,128)S(1)}, u32[]{:S(2)}, u32[]{:S(2)}) %collective-permute-start.2) | collective-permute-done | bytes 4128 | tf_op jit(solution)/shard_map/ppermute | solution.py:681
  16.2 0.0 copy-done
  16.2 0.0 copy-done.3
  16.2 0.0 copy-done.12
  16.2 2.8 %states.2 = (bf16[128,2048]{1,0:T(8,128)(2,1)S(1)}, f32[16,16,8,128]{3,2,1,0:T(8,128)}, f32[2,16,8,128]{3,2,1,0:T(8,128)S(1)}, bf16[256,2048]{1,0:T(8,128)(2,1)}) custom-call(bf16[128,2048]{1,0:T(8,128)(2,1)S(1)} %get-tuple-element.25.refs_0_, bf16[256,2048]{1,0:T(8,128)(2,1)S(1)} %copy-done.3, f32[8,128]{1,0:T(8,128)S(1)} %add.6.refs_2_, ...), custom_call_target="tpu_custom_call" | custom-call | tf_op jit(solution)/shard_map/states/pallas_call | solution.py:66
  19.0 0.0 collective-permute-done.before_ref
  19.0 0.0 copy-done.2
  19.0 0.0 copy-done.7
  19.1 0.0 copy-done.8
  19.1 0.0 copy-done.11
  19.1 0.0 copy-done.1
  19.1 2.0 %lower.1 = (bf16[128,2048]{1,0:T(8,128)(2,1)S(1)}, f32[8,128]{1,0:T(8,128)S(1)}) custom-call(bf16[128,2048]{1,0:T(8,128)(2,1)S(1)} %collective-permute-done.before_ref, bf16[128,2048]{1,0:T(8,128)(2,1)S(1)} %get-tuple-element.29.here_ref, f32[128,2048]{1,0:T(8,128)S(1)} %get-tuple-element.30.even_ref, f32[128,2048]{1,0:T(8,128)S(1)} %get-tuple-element.31.cross_ref, ...), custom_call_target="tpu_custom_call" | custom-call | tf_op jit(solution)/shard_map/lower/pallas_call | solution.py:66
  21.0 0.0 copy-start.4
  21.1 0.1 collective-permute-start.3
  21.1 1.2 %collective-permute-done.3 = f32[8,128]{1,0:T(8,128)S(1)} collective-permute-done((f32[8,128]{1,0:T(8,128)S(1)}, f32[8,128]{1,0:T(8,128)S(1)}, u32[]{:S(2)}, u32[]{:S(2)}) %collective-permute-start.3) | collective-permute-done | bytes 4128 | tf_op jit(solution)/shard_map/ppermute | solution.py:677
  22.3 3.0 %collective-permute-start.4 = (f32[8,128]{1,0:T(8,128)S(1)}, f32[8,128]{1,0:T(8,128)S(1)}, u32[]{:S(2)}, u32[]{:S(2)}) collective-permute-start(f32[8,128]{1,0:T(8,128)S(1)} %add.7.refs_2_), channel_id=1, source_target_pairs={{0,2},{2,0},{1,3},{3,1},{4,6},{6,4},{5,7},{7,5},{8,10},{10,8},{9,1... | collective-permute-start | bytes 12296 | tf_op jit(solution)/shard_map/ppermute | solution.py:681
  25.3 2.1 %collective-permute-done.4.refs_3_ = f32[8,128]{1,0:T(8,128)S(1)} collective-permute-done((f32[8,128]{1,0:T(8,128)S(1)}, f32[8,128]{1,0:T(8,128)S(1)}, u32[]{:S(2)}, u32[]{:S(2)}) %collective-permute-start.4) | collective-permute-done | bytes 4128 | tf_op jit(solution)/shard_map/ppermute | solution.py:681
  27.4 3.1 %states.3 = (bf16[128,2048]{1,0:T(8,128)(2,1)S(1)}, f32[16,16,8,128]{3,2,1,0:T(8,128)S(1)}, bf16[8,16,2048]{2,1,0:T(8,128)(2,1)}, bf16[256,2048]{1,0:T(8,128)(2,1)}) custom-call(bf16[128,2048]{1,0:T(8,128)(2,1)S(1)} %get-tuple-element.33.refs_0_, bf16[256,2048]{1,0:T(8,128)(2,1)S(1)} %copy-done.3, ...), custom_call_target="tpu_custom_call", output_to_operand_aliasing={{3}: (7, {})} | custom-call | tf_op jit(solution)/shard_map/states/pallas_call | solution.py:66
  30.5 0.0 copy-start.5
  30.5 1.0 %copy-done.5 = f32[16,16,8,128]{3,2,1,0:T(8,128)} copy-done((f32[16,16,8,128]{3,2,1,0:T(8,128)}, f32[16,16,8,128]{3,2,1,0:T(8,128)S(1)}, u32[]{:S(2)}) %copy-start.5) | copy-done | bytes 1048600
  31.5 0.8 %copy-done.9 = bf16[128,2048]{1,0:T(8,128)(2,1)} copy-done((bf16[128,2048]{1,0:T(8,128)(2,1)}, bf16[128,2048]{1,0:T(8,128)(2,1)S(1)}, u32[]{:S(2)}) %copy-start.9) | copy-done | bytes 524312
  32.3 8.3 %all-to-all-start = ((bf16[8,16,2048]{2,1,0:T(8,128)(2,1)}), bf16[8,16,2048]{2,1,0:T(8,128)(2,1)S(1)}, u32[]{:S(2)}, u32[]{:S(2)}) async-start(bf16[8,16,2048]{2,1,0:T(8,128)(2,1)} %get-tuple-element.38), calls=%async_computation | async-start | bytes 1048576 | tf_op jit(solution)/shard_map/all_to_all | solution.py:739
  40.6 1.2 %copy-done.6 = f32[16,16,8,128]{3,2,1,0:T(8,128)S(1)} copy-done((f32[16,16,8,128]{3,2,1,0:T(8,128)S(1)}, f32[16,16,8,128]{3,2,1,0:T(8,128)}, u32[]{:S(2)}) %copy-start.6) | copy-done | bytes 1048600
  41.8 2.8 %prefix.1.prefix_ref = f32[16,2,16,8,128]{4,3,2,1,0:T(8,128)S(1)} custom-call(f32[16,16,8,128]{3,2,1,0:T(8,128)S(1)} %copy-done.6, f32[16,16,8,128]{3,2,1,0:T(8,128)} %get-tuple-element.42.far_high_ref, f32[16,2048]{1,0:T(8,128)S(1)} %copy-done, f32[16,2048]{1,0:T(8,128)S(1)} %copy-done.4), custom_call_target="tpu_custom_call" | custom-call | tf_op jit(solution)/shard_map/prefix/pallas_call | solution.py:66
  44.6 3.0 %short.1.near_ref = f32[16,256,128]{2,1,0:T(8,128)} custom-call(bf16[128,2048]{1,0:T(8,128)(2,1)S(1)} %copy-done.10, bf16[128,2048]{1,0:T(8,128)(2,1)S(1)} %get-tuple-element.40.high_ref, f32[16,2048]{1,0:T(8,128)S(1)} %copy-done, f32[16,2048]{1,0:T(8,128)S(1)} %copy-done.4, f32[1,2048]{1,0:T(1,128)S(1)} %bitcast.7), custom_call_target="tpu_custom_call" | custom-call | tf_op jit(solution)/shard_map/short/pallas_call | solution.py:66
  47.6 1.8 %all-to-all-done.state_ref = bf16[8,16,2048]{2,1,0:T(8,128)(2,1)S(1)} async-done(((bf16[8,16,2048]{2,1,0:T(8,128)(2,1)}), bf16[8,16,2048]{2,1,0:T(8,128)(2,1)S(1)}, u32[]{:S(2)}, u32[]{:S(2)}) %all-to-all-start) | async-done | bytes 524320 | tf_op jit(solution)/shard_map/all_to_all | solution.py:739
  49.5 0.3 group.1
  49.7 4.7 %collective-permute-start.7 = (bf16[16,2048]{1,0:T(8,128)(2,1)S(1)}, bf16[16,2048]{1,0:T(8,128)(2,1)S(1)}, u32[]{:S(2)}, u32[]{:S(2)}) collective-permute-start(bf16[16,2048]{1,0:T(8,128)(2,1)S(1)} %get-tuple-element.47), channel_id=1, source_target_pairs={{0,96},{4,100},{8,104},{12,108},{16,112},{20,116},{24,120},{28,124... | collective-permute-start | bytes 196616 | tf_op jit(solution)/shard_map/ppermute | solution.py:747
  54.4 1.3 %collective-permute-start.6 = (bf16[16,2048]{1,0:T(8,128)(2,1)S(1)}, bf16[16,2048]{1,0:T(8,128)(2,1)S(1)}, u32[]{:S(2)}, u32[]{:S(2)}) collective-permute-start(bf16[16,2048]{1,0:T(8,128)(2,1)S(1)} %get-tuple-element.47), channel_id=1, source_target_pairs={{0,64},{4,68},{8,72},{12,76},{16,80},{20,84},{24,88},{28,92},{32,9... | collective-permute-start | bytes 196616 | tf_op jit(solution)/shard_map/ppermute | solution.py:747
  55.7 2.8 %collective-permute-start.5 = (bf16[16,2048]{1,0:T(8,128)(2,1)S(1)}, bf16[16,2048]{1,0:T(8,128)(2,1)S(1)}, u32[]{:S(2)}, u32[]{:S(2)}) collective-permute-start(bf16[16,2048]{1,0:T(8,128)(2,1)S(1)} %get-tuple-element.47), channel_id=1, source_target_pairs={{0,32},{4,36},{8,40},{12,44},{16,48},{20,52},{24,56},{28,60},{32,6... | collective-permute-start | bytes 196616 | tf_op jit(solution)/shard_map/ppermute | solution.py:747
  58.5 0.0 collective-permute-done.7.three_ref
  58.5 0.0 collective-permute-done.6.two_ref
  58.5 1.9 %collective-permute-done.5.one_ref = bf16[16,2048]{1,0:T(8,128)(2,1)S(1)} collective-permute-done((bf16[16,2048]{1,0:T(8,128)(2,1)S(1)}, bf16[16,2048]{1,0:T(8,128)(2,1)S(1)}, u32[]{:S(2)}, u32[]{:S(2)}) %collective-permute-start.5) | collective-permute-done | bytes 65568 | tf_op jit(solution)/shard_map/ppermute | solution.py:747
  60.4 4.7 %output.1 = bf16[256,2048]{1,0:T(8,128)(2,1)} custom-call(f32[16,256,128]{2,1,0:T(8,128)} %short.1.near_ref, f32[16,2,16,8,128]{4,3,2,1,0:T(8,128)S(1)} %prefix.1.prefix_ref, f32[16,2048]{1,0:T(8,128)S(1)} %get-tuple-element.46.before_ref, bf16[16,2048]{1,0:T(8,128)(2,1)S(1)} %collective-permute-done.5.one_ref, ...), custom_call_target="tpu_custom_call" | custom-call | tf_op jit(solution)/shard_map/output/pallas_call | solution.py:66
  (9 shorter events, 0.0 us)
Async XLA Ops:
  1.9 17.1 %collective-permute-start = (bf16[128,2048]{1,0:T(8,128)(2,1)S(1)}, bf16[128,2048]{1,0:T(8,128)(2,1)S(1)}, u32[]{:S(2)}, u32[]{:S(2)}) collective-permute-start(bf16[128,2048]{1,0:T(8,128)(2,1)S(1)} %slice_multiply_fusion.here_ref), channel_id=1, source_target_pairs={{0,4},{4,8},{8,12},{12,16},{16,20},{20,24},{24,28},{28,32},{32,36}... | collective-permute-start | bytes 1572872 | tf_op jit(solution)/shard_map/ppermute | solution.py:709
  5.9 10.3 %copy-start = (f32[16,2048]{1,0:T(8,128)S(1)}, f32[16,2048]{1,0:T(8,128)}, u32[]{:S(2)}) copy-start(f32[16,2048]{1,0:T(8,128)} %rate_ref.7) | copy-start | bytes 393220
  5.9 10.3 %copy-start.3 = (bf16[256,2048]{1,0:T(8,128)(2,1)S(1)}, bf16[256,2048]{1,0:T(8,128)(2,1)}, u32[]{:S(2)}) copy-start(bf16[256,2048]{1,0:T(8,128)(2,1)} %refs_1_.3) | copy-start | bytes 3145732
  5.9 10.3 %copy-start.12 = (f32[2048]{0:T(1024)S(1)}, f32[2048]{0:T(1024)}, u32[]{:S(2)}) copy-start(f32[2048]{0:T(1024)} %param.20) | copy-start | bytes 24580
  5.9 13.1 %copy-start.2 = (bf16[256,2048]{1,0:T(8,128)(2,1)S(1)}, bf16[256,2048]{1,0:T(8,128)(2,1)}, u32[]{:S(2)}) copy-start(bf16[256,2048]{1,0:T(8,128)(2,1)} %resid_ref.1) | copy-start | bytes 3145732
  5.9 13.1 %copy-start.7 = (bf16[512,256]{1,0:T(8,128)(2,1)S(1)}, bf16[512,256]{1,0:T(8,128)(2,1)}, u32[]{:S(2)}) copy-start(bf16[512,256]{1,0:T(8,128)(2,1)} %constant.4.clone.fwd_far.fwd_ref) | copy-start | bytes 786436
  5.9 13.1 %copy-start.8 = (bf16[256,256]{1,0:T(8,128)(2,1)S(1)}, bf16[256,256]{1,0:T(8,128)(2,1)}, u32[]{:S(2)}) copy-start(bf16[256,256]{1,0:T(8,128)(2,1)} %constant.5.clone.bwd_far.bwd_ref) | copy-start | bytes 393220
  5.9 13.1 %copy-start.11 = (f32[2048]{0:T(1024)S(1)}, f32[2048]{0:T(1024)}, u32[]{:S(2)}) copy-start(f32[2048]{0:T(1024)} %param.19) | copy-start | bytes 24580
  9.8 9.3 %copy-start.1 = (bf16[256,2048]{1,0:T(8,128)(2,1)S(1)}, bf16[256,2048]{1,0:T(8,128)(2,1)}, u32[]{:S(2)}) copy-start(bf16[256,2048]{1,0:T(8,128)(2,1)} %query_ref.2) | copy-start | bytes 3145732
  9.8 1.2 %collective-permute-start.1 = (f32[8,128]{1,0:T(8,128)S(1)}, f32[8,128]{1,0:T(8,128)S(1)}, u32[]{:S(2)}, u32[]{:S(2)}) collective-permute-start(f32[8,128]{1,0:T(8,128)S(1)} %get-tuple-element.26), channel_id=1, source_target_pairs={{0,1},{1,0},{2,3},{3,2},{4,5},{5,4},{6,7},{7,6},{8,9},{9,8},{10,11... | collective-permute-start | bytes 12296 | tf_op jit(solution)/shard_map/ppermute | solution.py:677
  11.1 5.1 %collective-permute-start.2 = (f32[8,128]{1,0:T(8,128)S(1)}, f32[8,128]{1,0:T(8,128)S(1)}, u32[]{:S(2)}, u32[]{:S(2)}) collective-permute-start(f32[8,128]{1,0:T(8,128)S(1)} %add.6.refs_2_), channel_id=1, source_target_pairs={{0,2},{2,0},{1,3},{3,1},{4,6},{6,4},{5,7},{7,5},{8,10},{10,8},{9,1... | collective-permute-start | bytes 12296 | tf_op jit(solution)/shard_map/ppermute | solution.py:681
  21.0 19.6 %copy-start.4 = (f32[16,2048]{1,0:T(8,128)S(1)}, f32[16,2048]{1,0:T(8,128)}, u32[]{:S(2)}) copy-start(f32[16,2048]{1,0:T(8,128)} %residue_ref.5) | copy-start | bytes 393220
  21.1 1.2 %collective-permute-start.3 = (f32[8,128]{1,0:T(8,128)S(1)}, f32[8,128]{1,0:T(8,128)S(1)}, u32[]{:S(2)}, u32[]{:S(2)}) collective-permute-start(f32[8,128]{1,0:T(8,128)S(1)} %get-tuple-element.34), channel_id=1, source_target_pairs={{0,1},{1,0},{2,3},{3,2},{4,5},{5,4},{6,7},{7,6},{8,9},{9,8},{10,11... | collective-permute-start | bytes 12296 | tf_op jit(solution)/shard_map/ppermute | solution.py:677
  22.3 5.1 %collective-permute-start.4 = (f32[8,128]{1,0:T(8,128)S(1)}, f32[8,128]{1,0:T(8,128)S(1)}, u32[]{:S(2)}, u32[]{:S(2)}) collective-permute-start(f32[8,128]{1,0:T(8,128)S(1)} %add.7.refs_2_), channel_id=1, source_target_pairs={{0,2},{2,0},{1,3},{3,1},{4,6},{6,4},{5,7},{7,5},{8,10},{10,8},{9,1... | collective-permute-start | bytes 12296 | tf_op jit(solution)/shard_map/ppermute | solution.py:681
  30.5 1.0 %copy-start.5 = (f32[16,16,8,128]{3,2,1,0:T(8,128)}, f32[16,16,8,128]{3,2,1,0:T(8,128)S(1)}, u32[]{:S(2)}) copy-start(f32[16,16,8,128]{3,2,1,0:T(8,128)S(1)} %get-tuple-element.41.low_ref) | copy-start | bytes 3145732
  31.5 0.8 %copy-start.9 = (bf16[128,2048]{1,0:T(8,128)(2,1)}, bf16[128,2048]{1,0:T(8,128)(2,1)S(1)}, u32[]{:S(2)}) copy-start(bf16[128,2048]{1,0:T(8,128)(2,1)S(1)} %get-tuple-element.39.low_ref) | copy-start | bytes 1572868
  32.3 17.1 %all-to-all-start = ((bf16[8,16,2048]{2,1,0:T(8,128)(2,1)}), bf16[8,16,2048]{2,1,0:T(8,128)(2,1)S(1)}, u32[]{:S(2)}, u32[]{:S(2)}) async-start(bf16[8,16,2048]{2,1,0:T(8,128)(2,1)} %get-tuple-element.38), calls=%async_computation | async-start | bytes 1048576 | tf_op jit(solution)/shard_map/all_to_all | solution.py:739
  40.6 1.2 %copy-start.6 = (f32[16,16,8,128]{3,2,1,0:T(8,128)S(1)}, f32[16,16,8,128]{3,2,1,0:T(8,128)}, u32[]{:S(2)}) copy-start(f32[16,16,8,128]{3,2,1,0:T(8,128)} %copy-done.5) | copy-start | bytes 3145732
  41.8 2.8 %copy-start.10 = (bf16[128,2048]{1,0:T(8,128)(2,1)S(1)}, bf16[128,2048]{1,0:T(8,128)(2,1)}, u32[]{:S(2)}) copy-start(bf16[128,2048]{1,0:T(8,128)(2,1)} %copy-done.9) | copy-start | bytes 1572868
  41.8 2.8 %copy-start.13 = (f32[2048]{0:T(1024)S(1)}, f32[2048]{0:T(1024)}, u32[]{:S(2)}) copy-start(f32[2048]{0:T(1024)} %param.25) | copy-start | bytes 24580
  49.7 8.8 %collective-permute-start.7 = (bf16[16,2048]{1,0:T(8,128)(2,1)S(1)}, bf16[16,2048]{1,0:T(8,128)(2,1)S(1)}, u32[]{:S(2)}, u32[]{:S(2)}) collective-permute-start(bf16[16,2048]{1,0:T(8,128)(2,1)S(1)} %get-tuple-element.47), channel_id=1, source_target_pairs={{0,96},{4,100},{8,104},{12,108},{16,112},{20,116},{24,120},{28,124... | collective-permute-start | bytes 196616 | tf_op jit(solution)/shard_map/ppermute | solution.py:747
  54.4 4.1 %collective-permute-start.6 = (bf16[16,2048]{1,0:T(8,128)(2,1)S(1)}, bf16[16,2048]{1,0:T(8,128)(2,1)S(1)}, u32[]{:S(2)}, u32[]{:S(2)}) collective-permute-start(bf16[16,2048]{1,0:T(8,128)(2,1)S(1)} %get-tuple-element.47), channel_id=1, source_target_pairs={{0,64},{4,68},{8,72},{12,76},{16,80},{20,84},{24,88},{28,92},{32,9... | collective-permute-start | bytes 196616 | tf_op jit(solution)/shard_map/ppermute | solution.py:747
  55.7 4.7 %collective-permute-start.5 = (bf16[16,2048]{1,0:T(8,128)(2,1)S(1)}, bf16[16,2048]{1,0:T(8,128)(2,1)S(1)}, u32[]{:S(2)}, u32[]{:S(2)}) collective-permute-start(bf16[16,2048]{1,0:T(8,128)(2,1)S(1)} %get-tuple-element.47), channel_id=1, source_target_pairs={{0,32},{4,36},{8,40},{12,44},{16,48},{20,52},{24,56},{28,60},{32,6... | collective-permute-start | bytes 196616 | tf_op jit(solution)/shard_map/ppermute | solution.py:747

commit v2 on v1

--- a/solution.py
+++ b/solution.py
@@ -294,19 +294,29 @@
     return pl.ds(pl.multiple_of(block * LANES, LANES), LANES)
 
 
+def swept(wide_ref, decay_ref):
+    decay = [row_of(decay_ref, m, pl.ds(0, LANES)) for m in range(decay_ref.shape[0])]
+    held = None
+    for i in range(STEPS):
+        step = wide_ref[pl.ds(i, SUB, stride=STEPS), :]
+        held = [step] * len(decay) if i == 0 else [h * d + step for h, d in zip(held, decay)]
+    return held
+
+
 def state_kernel(row_start, total_channels, last, *refs):
     part_ref, key_ref, near_ref, far_ref, gain_ref, rate_ref = refs[:6]
     if last:
         later_ref = refs[6]
-        refs = refs[2:]
-    value_ref, end_ref, state_ref, joined_ref, wide_ref, scale_ref, decay_ref, sems = refs[6:14]
-    held_ref = end_ref if last else refs[14]
+        value_ref, state_ref, joined_ref, wide_ref, scale_ref, decay_ref, sems = refs[8:]
+        made_ref = value_ref
+    else:
+        value_ref, state_ref, joined_ref, end_ref = refs[6:10]
+        wide_ref, scale_ref, decay_ref, sems, made_ref, held_ref = refs[10:]
     join = pltpu.make_async_copy(
         part_ref, joined_ref.at[pl.ds(row_start, HALF), :], sems.at[0]
     )
     join.start()
-    modes = rate_ref.shape[0]
-    blocks = end_ref.shape[0]
+    modes, channels = rate_ref.shape
     rows = pl.ds(row_start, HALF)
     scale = lax.rsqrt((near_ref[...] + far_ref[...]) / total_channels + 1e-05)
     scale_ref[...] = jnp.broadcast_to(scale[:1], (HALF, HALF)).T
@@ -319,20 +329,15 @@
             * scale_ref[...]
             * gain_ref[:, cols]
         ).astype(jnp.bfloat16)
-        value_ref[:, cols] = value
+        made_ref[:, cols] = value
         wide_ref[side] = value.astype(jnp.float32)
-        every = pl.ds(0, LANES)
-        decay = [row_of(decay_ref.at[side], m, every) for m in range(modes)]
-        held = [None] * modes
-        for i in range(STEPS):
-            step = wide_ref[side, pl.ds(i, SUB, stride=STEPS), :]
+        held = swept(wide_ref.at[side], decay_ref.at[side])
+        if not last:
             for m in range(modes):
-                held[m] = step if i == 0 else held[m] * decay[m] + step
+                held_ref[block, m] = held[m]
+            pltpu.make_async_copy(held_ref.at[block], end_ref.at[block], sems.at[1]).start()
+            pltpu.make_async_copy(made_ref.at[:, cols], value_ref.at[:, cols], sems.at[2]).start()
         remaining = (sublane_iota() - (SUB - 1)).astype(jnp.float32) * float(STEPS)
-        for m in range(modes):
-            held_ref[block, m] = held[m]
-        if not last:
-            pltpu.make_async_copy(held_ref.at[block], end_ref.at[block], sems.at[1]).start()
         tiles = []
         for group in range(modes // SUB):
             span = range(group * SUB, (group + 1) * SUB)
@@ -351,10 +356,11 @@
             for group, state in enumerate(tiles):
                 state_ref[group, block] = state
 
-    lane_blocks(blocks * LANES, body)
+    lane_blocks(channels, body)
     join.wait()
     if not last:
         pltpu.make_async_copy(held_ref, end_ref, sems.at[1]).wait()
+        pltpu.make_async_copy(made_ref, value_ref, sems.at[2]).wait()
 
 
 def gathered_sums(values):
@@ -375,31 +381,31 @@
     modes = rates.shape[0]
     blocks = channels // LANES
     ends = (blocks, modes, SUB, LANES)
-    joined = shape_of((2 * HALF, channels), jnp.bfloat16)
+    outputs = [
+        shape_of(part.shape, jnp.bfloat16),
+        shape_of((GROUP, modes, channels), jnp.bfloat16)
+        if last
+        else shape_of((modes // SUB, blocks, SUB, LANES), jnp.float32),
+        shape_of((2 * HALF, channels), jnp.bfloat16),
+    ]
     scratch = [
         pltpu.VMEM((2, HALF, LANES), jnp.float32),
         pltpu.VMEM((HALF, HALF), jnp.float32),
         pltpu.VMEM((2, modes, LANES), jnp.float32),
-        pltpu.SemaphoreType.DMA((2,)),
+        pltpu.SemaphoreType.DMA((3,)),
     ]
     if not last:
-        scratch += [pltpu.VMEM(ends, jnp.float32)]
+        outputs += [shape_of(ends, jnp.float32)]
+        scratch += [pltpu.VMEM(part.shape, jnp.bfloat16), pltpu.VMEM(ends, jnp.float32)]
     return local_call(
         functools.partial(state_kernel, row_start, total_channels, len(last)),
         "states",
-        [
-            shape_of(part.shape, jnp.bfloat16),
-            shape_of(ends, jnp.float32),
-            shape_of((GROUP, modes, channels), jnp.bfloat16)
-            if last
-            else shape_of((modes // SUB, blocks, SUB, LANES), jnp.float32),
-            joined,
-        ],
+        outputs,
         (part, key, near, far, gain, rates, *last),
         scratch,
         far_in=(7,) if last else (),
-        far_out=(3,) if last else (1, 3),
-        aliases={7: 3} if last else {},
+        far_out=(2,) if last else (0, 2, 3),
+        aliases={7: 2} if last else {},
     )
 
 
@@ -418,17 +424,19 @@
             if source > 0:
                 before = jnp.where(member == source, held, before)
             held = held * decay + state_ref[source, :, cols].astype(jnp.float32)
-        total_ref[:, cols] = held.astype(jnp.bfloat16)
+        total = held.astype(jnp.bfloat16)
+        for level in range(total_ref.shape[0]):
+            total_ref[level, :, cols] = total
         before_ref[:, cols] = before
 
     lane_blocks(rate_ref.shape[1], body)
 
 
-def group_scan(rates, states, span):
+def group_scan(rates, states, span, levels):
     return local_call(
         functools.partial(group_kernel, float(span)),
         "group",
-        [shape_of(rates.shape, jnp.bfloat16), shape_of(rates.shape, jnp.float32)],
+        [shape_of((levels, *rates.shape), jnp.bfloat16), shape_of(rates.shape, jnp.float32)],
         (rates, states),
     )
 
@@ -444,12 +452,70 @@
     return terms[0]
 
 
-def short_kernel(
-    low_ref, high_ref, rate_ref, residue_ref, skip_ref, near_ref, wide_ref, tap_ref, made_ref, sem
+def weights_of(residue_ref, rate_ref):
+    rates = rate_ref[...]
+    return residue_ref[...] * jnp.sqrt(rates) * jnp.exp(-rates)
+
+
+def inner_kernel(
+    low_ref,
+    far_value_ref,
+    far_end_ref,
+    rate_ref,
+    residue_ref,
+    skip_ref,
+    near_ref,
+    out_ref,
+    weight_ref,
+    wide_ref,
+    decay_ref,
+    tap_ref,
+    made_ref,
+    high_ref,
+    end_ref,
+    sems,
+    value_sem,
+    near_sem,
 ):
-    modes = rate_ref.shape[0]
-
-    def body(block, cols, side):
+    modes, channels = rate_ref.shape
+    blocks = channels // LANES
+
+    def arriving(block):
+        return pltpu.make_async_copy(far_end_ref.at[block], end_ref.at[block], sems.at[block])
+
+    for block in range(blocks):
+        arriving(block).start()
+    fetch = pltpu.make_async_copy(far_value_ref, high_ref, value_sem)
+    fetch.start()
+    weight_ref[...] = weights_of(residue_ref, rate_ref)
+
+    def joined(run, spans):
+        for span, factor in zip((1, 2, 4), spans):
+            run = run + factor * shifted_down(run, span)
+        return run
+
+    def prefix_body(block, cols, side):
+        decay_ref[side] = jnp.exp(-rate_ref[:, cols])
+        wide_ref[side, 0] = low_ref[:, cols].astype(jnp.float32)
+        lows = swept(wide_ref.at[side, 0], decay_ref.at[side])
+        arriving(block).wait()
+        position = sublane_iota().astype(jnp.float32) * float(-STEPS)
+        for m in range(modes):
+            rate = row_of(rate_ref, m, cols)
+            weight = row_of(weight_ref, m, cols)
+            spans = [jnp.exp(rate * float(-STEPS * span)) for span in (1, 2, 4)]
+            run = joined(lows[m], spans)
+            out_ref[block, 0, m] = shifted_down(run, 1) * weight
+            carried = jnp.broadcast_to(run[SUB - 1 :], (SUB, LANES))
+            run = joined(end_ref[block, m], spans)
+            out_ref[block, 1, m] = (
+                shifted_down(run, 1) + jnp.exp(rate * position) * carried
+            ) * weight
+
+    lane_blocks(channels, prefix_body)
+    fetch.wait()
+
+    def short_body(block, cols, side):
         for start in range(0, STEPS, SUB):
             offset = (sublane_iota() + start).astype(jnp.float32)
             terms = []
@@ -472,82 +538,35 @@
                     sums[i] = term if k == 0 else sums[i] + term
             for i in range(STEPS):
                 made_ref[block, pl.ds((half * STEPS + i) * SUB, SUB), :] = sums[i]
-        pltpu.make_async_copy(made_ref.at[block], near_ref.at[block], sem).start()
-
-    lane_blocks(low_ref.shape[1], body)
-    pltpu.make_async_copy(made_ref, near_ref, sem).wait()
-
-
-def short_part(low, high, rates, residues, skip):
-    shape = (low.shape[1] // LANES, 2 * HALF, LANES)
+        pltpu.make_async_copy(made_ref.at[block], near_ref.at[block], near_sem).start()
+
+    lane_blocks(channels, short_body)
+    pltpu.make_async_copy(made_ref, near_ref, near_sem).wait()
+
+
+def inner_part(low, high, high_end, rates, residues, skip):
+    modes, channels = rates.shape
+    blocks = channels // LANES
+    near = shape_of((blocks, 2 * HALF, LANES), jnp.float32)
     return local_call(
-        short_kernel,
-        "short",
-        shape_of(shape, jnp.float32),
-        (low, high, rates, residues, skip),
+        inner_kernel,
+        "inner",
+        [near, shape_of((blocks, 2, modes, SUB, LANES), jnp.float32)],
+        (low, high, high_end, rates, residues, skip),
         [
+            pltpu.VMEM(rates.shape, jnp.float32),
             pltpu.VMEM((2, 2, HALF, LANES), jnp.float32),
+            pltpu.VMEM((2, modes, LANES), jnp.float32),
             pltpu.VMEM((2, STEPS, LANES), jnp.float32),
-            pltpu.VMEM(shape, jnp.float32),
+            pltpu.VMEM(near.shape, jnp.float32),
+            pltpu.VMEM(high.shape, high.dtype),
+            pltpu.VMEM(high_end.shape, high_end.dtype),
+            pltpu.SemaphoreType.DMA((blocks,)),
+            pltpu.SemaphoreType.DMA(()),
             pltpu.SemaphoreType.DMA(()),
         ],
+        far_in=(1, 2),
         far_out=(0,),
-    )
-
-
-def weights_of(residue_ref, rate_ref):
-    rates = rate_ref[...]
-    return residue_ref[...] * jnp.sqrt(rates) * jnp.exp(-rates)
-
-
-def prefix_kernel(
-    low_ref, far_high_ref, rate_ref, residue_ref, out_ref, weight_ref, high_ref, sems
-):
-    modes = rate_ref.shape[0]
-    blocks = low_ref.shape[0]
-
-    def arriving(block):
-        return pltpu.make_async_copy(far_high_ref.at[block], high_ref.at[block], sems.at[block])
-
-    for block in range(blocks):
-        arriving(block).start()
-    weight_ref[...] = weights_of(residue_ref, rate_ref)
-
-    def body(block, cols, side):
-        arriving(block).wait()
-        for m in range(modes):
-            rate = row_of(rate_ref, m, cols)
-            weight = row_of(weight_ref, m, cols)
-            spans = [jnp.exp(rate * float(-STEPS * span)) for span in (1, 2, 4)]
-            run = low_ref[block, m]
-            for span, factor in zip((1, 2, 4), spans):
-                run = run + factor * shifted_down(run, span)
-            out_ref[block, 0, m] = shifted_down(run, 1) * weight
-            carried = jnp.broadcast_to(run[SUB - 1 :], (SUB, LANES))
-            run = high_ref[block, m]
-            for span, factor in zip((1, 2, 4), spans):
-                run = run + factor * shifted_down(run, span)
-            position = sublane_iota().astype(jnp.float32) * float(-STEPS)
-            out_ref[block, 1, m] = (
-                shifted_down(run, 1) + jnp.exp(rate * position) * carried
-            ) * weight
-
-    lane_blocks(blocks * LANES, body)
-
-
-def prefixes(low, high, rates, residues):
-    blocks, modes = low.shape[:2]
-    return local_call(
-        prefix_kernel,
-        "prefix",
-        shape_of((blocks, 2, modes, SUB, LANES), low.dtype),
-        (low, high, rates, residues),
-        [
-            pltpu.VMEM(rates.shape, rates.dtype),
-            pltpu.VMEM(high.shape, high.dtype),
-            pltpu.SemaphoreType.DMA((blocks,)),
-        ],
-        far_in=(1,),
     )
 
 
@@ -556,9 +575,7 @@
     near_ref,
     prefix_ref,
     before_ref,
-    one_ref,
-    two_ref,
-    three_ref,
+    totals_ref,
     rate_ref,
     residue_ref,
     query_ref,
@@ -592,9 +609,12 @@
     member = member_index().astype(jnp.float32)
     span = float(2 * HALF)
     level = jnp.exp(rates * (-span * GROUP))
-    earlier = one_ref[...].astype(jnp.float32) + level * (
-        two_ref[...].astype(jnp.float32) + level * three_ref[...].astype(jnp.float32)
-    )
+    held = jnp.zeros_like(rates)
+    earlier = held
+    row = lax.div(lax.axis_index("ctx"), GROUP)
+    for source in range(totals_ref.shape[0] - 1):
+        held = held * level + totals_ref[source].astype(jnp.float32)
+        earlier = jnp.where(row == source + 1, held, earlier)
     start = before_ref[...] + jnp.exp(rates * (-span * member)) * earlier
     weight_ref[...] = weights_of(residue_ref, rate_ref) * start
 
@@ -656,7 +676,7 @@
         functools.partial(output_kernel, 2),
         "output",
         shape_of(query.shape, jnp.bfloat16),
-        (near, prefix, before, *earlier, rates, residues, query),
+        (near, prefix, before, earlier, rates, residues, query),
         [
             pltpu.VMEM(near.shape, jnp.float32),
             pltpu.VMEM(query.shape, jnp.bfloat16),
@@ -668,7 +688,7 @@
             pltpu.SemaphoreType.DMA((2, blocks)),
             pltpu.SemaphoreType.DMA(()),
         ],
-        far_in=(0, 8),
+        far_in=(0, 6),
         far_out=(0,),
     )
 
@@ -713,7 +733,7 @@
     near_high = summed_with_pair(square_high)
     far_high = across_pairs(near_high)
     total_channels = channels * lax.axis_size("tp")
-    value_high, end_high, state_high, residual_out = half_states(
+    value_high, state_high, residual_out, end_high = half_states(
         high, key_two, near_high, far_high, gain_row, decay_rates, HALF, total_channels
     )
     before, state_high = lax.optimization_barrier((before, state_high))
@@ -722,7 +742,7 @@
     )
     near_low = summed_with_pair(square_low)
     far_low = across_pairs(near_low)
-    value_low, end_low, state, residual_out = half_states(
+    value_low, state, residual_out = half_states(
         low,
         key_two,
         near_low,
@@ -739,14 +759,15 @@
     gathered = lax.all_to_all(
         state, "ctx", split_axis=0, concat_axis=0, tiled=True, axis_index_groups=members
     )
-    near = short_part(value_low, value_high, decay_rates, residues, skip_long)
-    prefix = prefixes(end_low, end_high, decay_rates, residues)
+    near, prefix = inner_part(
+        value_low, value_high, end_high, decay_rates, residues, skip_long
+    )
     gathered, near, prefix = lax.optimization_barrier((gathered, near, prefix))
-    total, before_here = group_scan(decay_rates, gathered, rows)
-    earlier = [
-        lax.ppermute(total, "ctx", [(d, d + far) for d in range(count - far)])
-        for far in range(GROUP, count, GROUP)
-    ]
+    total, before_here = group_scan(decay_rates, gathered, rows, count // GROUP)
+    columns = [list(range(first, count, GROUP)) for first in range(GROUP)]
+    earlier = lax.all_to_all(
+        total, "ctx", split_axis=0, concat_axis=0, tiled=True, axis_index_groups=columns
+    )
     result = long_output(
         near, prefix, before_here, earlier, decay_rates, residues, query_two
     )

time: 66.2 us -> 63.8 us (0.964); the launches traced: 65.1 us -> 63.5 us
  blocking collectives: 0 us -> 10.8 us
  starting transfers between devices: 27.2 us -> 18.5 us
  local copies, waits for them, and re-layouts: 3.08 us -> 0.06 us
  waiting for transfers between devices: 10.2 us -> 8.43 us
  Pallas kernels: 22.5 us -> 23.6 us
    all_to_all x0 -> x1, blocking collectives: none -> 10.8 us  [on_device(): lax.all_to_all(total, 'ctx', split_axis=0, concat_axis=0, tiled=True, axi...]
    ppermute x3 -> x0, starting transfers between devices: 8.76 us -> none  [on_device(): lax.ppermute(total, 'ctx', [(d, d + far) for d in range(count - far)])]
    unnamed x28 -> x20, local copies, waits for them, and re-layouts: 3.08 us -> 0.06 us
    ppermute x3 -> x0, waiting for transfers between devices: 1.87 us -> none  [on_device(): lax.ppermute(total, 'ctx', [(d, d + far) for d in range(count - far)])]
    pallas_call x8 -> x7, Pallas kernels: 22.5 us -> 23.6 us  [local_call(): call(*[pltpu.with_memory_space_constraint(operand, HBM if k in far_in els...]
  transfers between devices with their start and end apart: 9 -> 6, of which waited for: 6 -> 5; matrix products, arithmetic and copies ran while one was open for 0% -> 0% of each run, Pallas kernels for 19% -> 21%
where the time goes in v2:
time: 63.8 us; the launch traced here: 63.5 us
  Pallas kernels  23.6 us (37%)
  starting transfers between devices  18.5 us (29%)
  blocking collectives  10.8 us (17%)
  waiting for transfers between devices  8.43 us (13%)
  other arithmetic  1.26 us (2%)
  between operations  0.85 us (1%)
    pallas_call x7, Pallas kernels, local_call(): call(*[pltpu.with_memory_space_constraint(operand, HBM if k in far_in els...  23.6 us
    all_to_all x1, blocking collectives, on_device(): lax.all_to_all(total, 'ctx', split_axis=0, concat_axis=0, tiled=True, axi...  10.8 us
    all_to_all x1, starting transfers between devices, on_device(): lax.all_to_all(state, 'ctx', split_axis=0, concat_axis=0, tiled=True, axi...  8.29 us
    ppermute x2, starting transfers between devices, across_pairs(): return lax.ppermute(value, 'tp', [(0, 2), (2, 0), (1, 3), (3, 1)])  6.04 us
    ppermute x2, waiting for transfers between devices, across_pairs(): return lax.ppermute(value, 'tp', [(0, 2), (2, 0), (1, 3), (3, 1)])  4.18 us
    ppermute x1, starting transfers between devices, on_device(): lax.ppermute(product_high, 'ctx', [(d, d + 1) for d in range(count - 1)])  3.97 us
    ppermute x2, waiting for transfers between devices, summed_with_pair(): return value + lax.ppermute(value, 'tp', [(0, 1), (1, 0), (2, 3), (3, 2)])  2.31 us
    all_to_all x1, waiting for transfers between devices, on_device(): lax.all_to_all(state, 'ctx', split_axis=0, concat_axis=0, tiled=True, axi...  1.94 us
  transfers between devices with their start and end apart: 6, of which 5 were waited for; matrix products, arithmetic and copies ran while one was open for 0% of the time, Pallas kernels for 21%

profile of v2, /device:TPU:0, one launch (start us, length us, event | category | flops | bytes accessed | tf_op | source)
XLA Modules:
  0.0 63.5 jit_solution(8936237590658810517)
XLA Ops:
  0.6 1.3 %slice_multiply_fusion.here_ref = bf16[128,2048]{1,0:T(8,128)(2,1)S(1)} fusion(bf16[256,2048]{1,0:T(8,128)(2,1)} %value_far.1, bf16[256,2048]{1,0:T(8,128)(2,1)} %key_far.1), kind=kLoop, calls=%fused_computation | loop fusion | flops 262144 | bytes 1572864 | tf_op jit(solution)/shard_map/mul | solution.py:727
  1.9 4.0 %collective-permute-start = (bf16[128,2048]{1,0:T(8,128)(2,1)S(1)}, bf16[128,2048]{1,0:T(8,128)(2,1)S(1)}, u32[]{:S(2)}, u32[]{:S(2)}) collective-permute-start(bf16[128,2048]{1,0:T(8,128)(2,1)S(1)} %slice_multiply_fusion.here_ref), channel_id=1, source_target_pairs={{0,4},{4,8},{8,12},{12,16},{16,20},{20,24},{24,28},{28,32},{32,36}... | collective-permute-start | bytes 1572872 | tf_op jit(solution)/shard_map/ppermute | solution.py:729
  5.9 0.0 copy-start.2
  5.9 0.0 copy-start.3
  5.9 0.0 copy-start.8
  5.9 0.0 copy-start.1
  5.9 0.0 copy-start.4
  5.9 0.0 copy-start.6
  5.9 0.0 copy-start.7
  5.9 3.9 %upper.1 = (bf16[128,2048]{1,0:T(8,128)(2,1)S(1)}, f32[8,128]{1,0:T(8,128)S(1)}, bf16[128,2048]{1,0:T(8,128)(2,1)S(1)}, f32[128,2048]{1,0:T(8,128)S(1)}, f32[128...) custom-call(bf16[128,2048]{1,0:T(8,128)(2,1)S(1)} %slice_multiply_fusion.here_ref, bf16[256,2048]{1,0:T(8,128)(2,1)} %key_far.1, ...), custom_call_target="tpu_custom_call" | custom-call | tf_op jit(solution)/shard_map/upper/pallas_call | solution.py:66
  9.8 0.0 copy-start
  9.8 0.1 collective-permute-start.1
  9.9 1.2 %collective-permute-done.1 = f32[8,128]{1,0:T(8,128)S(1)} collective-permute-done((f32[8,128]{1,0:T(8,128)S(1)}, f32[8,128]{1,0:T(8,128)S(1)}, u32[]{:S(2)}, u32[]{:S(2)}) %collective-permute-start.1) | collective-permute-done | bytes 4128 | tf_op jit(solution)/shard_map/ppermute | solution.py:697
  11.1 3.0 %collective-permute-start.2 = (f32[8,128]{1,0:T(8,128)S(1)}, f32[8,128]{1,0:T(8,128)S(1)}, u32[]{:S(2)}, u32[]{:S(2)}) collective-permute-start(f32[8,128]{1,0:T(8,128)S(1)} %add.6.refs_2_), channel_id=1, source_target_pairs={{0,2},{2,0},{1,3},{3,1},{4,6},{6,4},{5,7},{7,5},{8,10},{10,8},{9,1... | collective-permute-start | bytes 12296 | tf_op jit(solution)/shard_map/ppermute | solution.py:701
  14.1 2.1 %collective-permute-done.2.refs_3_ = f32[8,128]{1,0:T(8,128)S(1)} collective-permute-done((f32[8,128]{1,0:T(8,128)S(1)}, f32[8,128]{1,0:T(8,128)S(1)}, u32[]{:S(2)}, u32[]{:S(2)}) %collective-permute-start.2) | collective-permute-done | bytes 4128 | tf_op jit(solution)/shard_map/ppermute | solution.py:701
  16.2 0.0 copy-done.2
  16.2 0.0 copy-done.3
  16.2 0.0 copy-done.8
  16.2 2.9 %states.2 = (bf16[128,2048]{1,0:T(8,128)(2,1)}, f32[2,16,8,128]{3,2,1,0:T(8,128)S(1)}, bf16[256,2048]{1,0:T(8,128)(2,1)}, f32[16,16,8,128]{3,2,1,0:T(8,128)}) custom-call(bf16[128,2048]{1,0:T(8,128)(2,1)S(1)} %get-tuple-element.26.refs_0_, bf16[256,2048]{1,0:T(8,128)(2,1)S(1)} %copy-done.2, f32[8,128]{1,0:T(8,128)S(1)} %add.6.refs_2_, ...), custom_call_target="tpu_custom_call" | custom-call | tf_op jit(solution)/shard_map/states/pallas_call | solution.py:66
  19.1 0.0 collective-permute-done.before_ref
  19.1 0.0 copy-done.1
  19.1 0.0 copy-done.4
  19.1 0.0 copy-done.6
  19.1 0.0 copy-done.7
  19.1 0.0 copy-done
  19.1 2.0 %lower.1 = (bf16[128,2048]{1,0:T(8,128)(2,1)S(1)}, f32[8,128]{1,0:T(8,128)S(1)}) custom-call(bf16[128,2048]{1,0:T(8,128)(2,1)S(1)} %collective-permute-done.before_ref, bf16[128,2048]{1,0:T(8,128)(2,1)S(1)} %get-tuple-element.30.here_ref, f32[128,2048]{1,0:T(8,128)S(1)} %get-tuple-element.31.even_ref, f32[128,2048]{1,0:T(8,128)S(1)} %get-tuple-element.32.cross_ref, ...), custom_call_target="tpu_custom_call" | custom-call | tf_op jit(solution)/shard_map/lower/pallas_call | solution.py:66
  21.1 0.0 copy-start.5
  21.1 0.0 copy-start.9
  21.1 0.1 collective-permute-start.3
  21.2 1.2 %collective-permute-done.3 = f32[8,128]{1,0:T(8,128)S(1)} collective-permute-done((f32[8,128]{1,0:T(8,128)S(1)}, f32[8,128]{1,0:T(8,128)S(1)}, u32[]{:S(2)}, u32[]{:S(2)}) %collective-permute-start.3) | collective-permute-done | bytes 4128 | tf_op jit(solution)/shard_map/ppermute | solution.py:697
  22.3 3.0 %collective-permute-start.4 = (f32[8,128]{1,0:T(8,128)S(1)}, f32[8,128]{1,0:T(8,128)S(1)}, u32[]{:S(2)}, u32[]{:S(2)}) collective-permute-start(f32[8,128]{1,0:T(8,128)S(1)} %add.7.refs_2_), channel_id=1, source_target_pairs={{0,2},{2,0},{1,3},{3,1},{4,6},{6,4},{5,7},{7,5},{8,10},{10,8},{9,1... | collective-permute-start | bytes 12296 | tf_op jit(solution)/shard_map/ppermute | solution.py:701
  25.4 2.1 %collective-permute-done.4.refs_3_ = f32[8,128]{1,0:T(8,128)S(1)} collective-permute-done((f32[8,128]{1,0:T(8,128)S(1)}, f32[8,128]{1,0:T(8,128)S(1)}, u32[]{:S(2)}, u32[]{:S(2)}) %collective-permute-start.4) | collective-permute-done | bytes 4128 | tf_op jit(solution)/shard_map/ppermute | solution.py:701
  27.5 3.1 %states.3 = (bf16[128,2048]{1,0:T(8,128)(2,1)S(1)}, bf16[8,16,2048]{2,1,0:T(8,128)(2,1)}, bf16[256,2048]{1,0:T(8,128)(2,1)}) custom-call(bf16[128,2048]{1,0:T(8,128)(2,1)S(1)} %get-tuple-element.34.refs_0_, bf16[256,2048]{1,0:T(8,128)(2,1)S(1)} %copy-done.2, f32[8,128]{1,0:T(8,128)S(1)} %add.7.refs_2_, ...), custom_call_target="tpu_custom_call", output_to_operand_aliasing={{2}: (7, {})} | custom-call | tf_op jit(solution)/shard_map/states/pallas_call | solution.py:66
  30.6 8.3 %all-to-all-start = ((bf16[8,16,2048]{2,1,0:T(8,128)(2,1)}), bf16[8,16,2048]{2,1,0:T(8,128)(2,1)S(1)}, u32[]{:S(2)}, u32[]{:S(2)}) async-start(bf16[8,16,2048]{2,1,0:T(8,128)(2,1)} %get-tuple-element.39), calls=%async_computation | async-start | bytes 1048576 | tf_op jit(solution)/shard_map/all_to_all | solution.py:759
  38.8 0.0 copy-done.5
  38.9 0.0 copy-done.9
  38.9 6.9 %inner.1 = (f32[16,256,128]{2,1,0:T(8,128)}, f32[16,2,16,8,128]{4,3,2,1,0:T(8,128)S(1)}) custom-call(bf16[128,2048]{1,0:T(8,128)(2,1)S(1)} %get-tuple-element.40.low_ref, bf16[128,2048]{1,0:T(8,128)(2,1)} %get-tuple-element.41.far_value_ref, f32[16,16,8,128]{3,2,1,0:T(8,128)} %get-tuple-element.42.far_end_ref, f32[16,2048]{1,0:T(8,128)S(1)} %copy-done.3, ...), custom_call_target="tpu_custom_call" | custom-call | tf_op jit(solution)/shard_map/inner/pallas_call | solution.py:66
  45.8 1.9 %all-to-all-done.state_ref = bf16[8,16,2048]{2,1,0:T(8,128)(2,1)S(1)} async-done(((bf16[8,16,2048]{2,1,0:T(8,128)(2,1)}), bf16[8,16,2048]{2,1,0:T(8,128)(2,1)S(1)}, u32[]{:S(2)}, u32[]{:S(2)}) %all-to-all-start) | async-done | bytes 524320 | tf_op jit(solution)/shard_map/all_to_all | solution.py:759
  47.7 0.3 group.1
  48.0 10.8 %all_to_all.10.totals_ref = bf16[4,16,2048]{2,1,0:T(8,128)(2,1)S(1)} all-to-all(bf16[4,16,2048]{2,1,0:T(8,128)(2,1)S(1)} %get-tuple-element.49), channel_id=1, replica_groups={{0,32,64,96},{4,36,68,100},{8,40,72,104},{12,44,76,108},{16,48,80,112},..., dimensions={0} | all-to-all | bytes 524288 | tf_op jit(solution)/shard_map/all_to_all | solution.py:768
  58.7 4.7 %output.1 = bf16[256,2048]{1,0:T(8,128)(2,1)} custom-call(f32[16,256,128]{2,1,0:T(8,128)} %get-tuple-element.45.near_ref, f32[16,2,16,8,128]{4,3,2,1,0:T(8,128)S(1)} %get-tuple-element.46.prefix_ref, f32[16,2048]{1,0:T(8,128)S(1)} %get-tuple-element.48.before_ref, bf16[4,16,2048]{2,1,0:T(8,128)(2,1)S(1)} %all_to_all.10.totals_ref, f32[16,2048]{1,0:T(8,128)S(1)} %copy-done.3, ...), custom_call_target="tpu_custom_call" | custom-call | tf_op jit(solution)/shard_map/output/pallas_call | solution.py:66
  (2 shorter events, 0.0 us)
Async XLA Ops:
  1.9 17.2 %collective-permute-start = (bf16[128,2048]{1,0:T(8,128)(2,1)S(1)}, bf16[128,2048]{1,0:T(8,128)(2,1)S(1)}, u32[]{:S(2)}, u32[]{:S(2)}) collective-permute-start(bf16[128,2048]{1,0:T(8,128)(2,1)S(1)} %slice_multiply_fusion.here_ref), channel_id=1, source_target_pairs={{0,4},{4,8},{8,12},{12,16},{16,20},{20,24},{24,28},{28,32},{32,36}... | collective-permute-start | bytes 1572872 | tf_op jit(solution)/shard_map/ppermute | solution.py:729
  5.9 10.3 %copy-start.2 = (bf16[256,2048]{1,0:T(8,128)(2,1)S(1)}, bf16[256,2048]{1,0:T(8,128)(2,1)}, u32[]{:S(2)}) copy-start(bf16[256,2048]{1,0:T(8,128)(2,1)} %refs_1_.3) | copy-start | bytes 3145732
  5.9 10.3 %copy-start.3 = (f32[16,2048]{1,0:T(8,128)S(1)}, f32[16,2048]{1,0:T(8,128)}, u32[]{:S(2)}) copy-start(f32[16,2048]{1,0:T(8,128)} %rate_ref.5) | copy-start | bytes 393220
  5.9 10.3 %copy-start.8 = (f32[2048]{0:T(1024)S(1)}, f32[2048]{0:T(1024)}, u32[]{:S(2)}) copy-start(f32[2048]{0:T(1024)} %param.20) | copy-start | bytes 24580
  5.9 13.2 %copy-start.1 = (bf16[256,2048]{1,0:T(8,128)(2,1)S(1)}, bf16[256,2048]{1,0:T(8,128)(2,1)}, u32[]{:S(2)}) copy-start(bf16[256,2048]{1,0:T(8,128)(2,1)} %resid_ref.1) | copy-start | bytes 3145732
  5.9 13.2 %copy-start.4 = (bf16[512,256]{1,0:T(8,128)(2,1)S(1)}, bf16[512,256]{1,0:T(8,128)(2,1)}, u32[]{:S(2)}) copy-start(bf16[512,256]{1,0:T(8,128)(2,1)} %constant.4.clone.fwd_far.fwd_ref) | copy-start | bytes 786436
  5.9 13.2 %copy-start.6 = (bf16[256,256]{1,0:T(8,128)(2,1)S(1)}, bf16[256,256]{1,0:T(8,128)(2,1)}, u32[]{:S(2)}) copy-start(bf16[256,256]{1,0:T(8,128)(2,1)} %constant.5.clone.bwd_far.bwd_ref) | copy-start | bytes 393220
  5.9 13.2 %copy-start.7 = (f32[2048]{0:T(1024)S(1)}, f32[2048]{0:T(1024)}, u32[]{:S(2)}) copy-start(f32[2048]{0:T(1024)} %param.19) | copy-start | bytes 24580
  9.8 9.3 %copy-start = (bf16[256,2048]{1,0:T(8,128)(2,1)S(1)}, bf16[256,2048]{1,0:T(8,128)(2,1)}, u32[]{:S(2)}) copy-start(bf16[256,2048]{1,0:T(8,128)(2,1)} %query_ref.2) | copy-start | bytes 3145732
  9.8 1.2 %collective-permute-start.1 = (f32[8,128]{1,0:T(8,128)S(1)}, f32[8,128]{1,0:T(8,128)S(1)}, u32[]{:S(2)}, u32[]{:S(2)}) collective-permute-start(f32[8,128]{1,0:T(8,128)S(1)} %get-tuple-element.27), channel_id=1, source_target_pairs={{0,1},{1,0},{2,3},{3,2},{4,5},{5,4},{6,7},{7,6},{8,9},{9,8},{10,11... | collective-permute-start | bytes 12296 | tf_op jit(solution)/shard_map/ppermute | solution.py:697
  11.1 5.1 %collective-permute-start.2 = (f32[8,128]{1,0:T(8,128)S(1)}, f32[8,128]{1,0:T(8,128)S(1)}, u32[]{:S(2)}, u32[]{:S(2)}) collective-permute-start(f32[8,128]{1,0:T(8,128)S(1)} %add.6.refs_2_), channel_id=1, source_target_pairs={{0,2},{2,0},{1,3},{3,1},{4,6},{6,4},{5,7},{7,5},{8,10},{10,8},{9,1... | collective-permute-start | bytes 12296 | tf_op jit(solution)/shard_map/ppermute | solution.py:701
  21.1 17.8 %copy-start.5 = (f32[16,2048]{1,0:T(8,128)S(1)}, f32[16,2048]{1,0:T(8,128)}, u32[]{:S(2)}) copy-start(f32[16,2048]{1,0:T(8,128)} %residue_ref.3) | copy-start | bytes 393220
  21.1 17.8 %copy-start.9 = (f32[2048]{0:T(1024)S(1)}, f32[2048]{0:T(1024)}, u32[]{:S(2)}) copy-start(f32[2048]{0:T(1024)} %param.25) | copy-start | bytes 24580
  21.1 1.2 %collective-permute-start.3 = (f32[8,128]{1,0:T(8,128)S(1)}, f32[8,128]{1,0:T(8,128)S(1)}, u32[]{:S(2)}, u32[]{:S(2)}) collective-permute-start(f32[8,128]{1,0:T(8,128)S(1)} %get-tuple-element.35), channel_id=1, source_target_pairs={{0,1},{1,0},{2,3},{3,2},{4,5},{5,4},{6,7},{7,6},{8,9},{9,8},{10,11... | collective-permute-start | bytes 12296 | tf_op jit(solution)/shard_map/ppermute | solution.py:697
  22.3 5.1 %collective-permute-start.4 = (f32[8,128]{1,0:T(8,128)S(1)}, f32[8,128]{1,0:T(8,128)S(1)}, u32[]{:S(2)}, u32[]{:S(2)}) collective-permute-start(f32[8,128]{1,0:T(8,128)S(1)} %add.7.refs_2_), channel_id=1, source_target_pairs={{0,2},{2,0},{1,3},{3,1},{4,6},{6,4},{5,7},{7,5},{8,10},{10,8},{9,1... | collective-permute-start | bytes 12296 | tf_op jit(solution)/shard_map/ppermute | solution.py:701
  30.6 17.1 %all-to-all-start = ((bf16[8,16,2048]{2,1,0:T(8,128)(2,1)}), bf16[8,16,2048]{2,1,0:T(8,128)(2,1)S(1)}, u32[]{:S(2)}, u32[]{:S(2)}) async-start(bf16[8,16,2048]{2,1,0:T(8,128)(2,1)} %get-tuple-element.39), calls=%async_computation | async-start | bytes 1048576 | tf_op jit(solution)/shard_map/all_to_all | solution.py:759

commit v3 on v2

--- a/solution.py
+++ b/solution.py
@@ -82,18 +82,28 @@
     return both[:count] + both[count:]
 
 
-def filtered_result(spec, taps, here, skip, query, resid, bwd):
+def joint_parts(spec, taps):
     even, cross, last = taps
     sig_even, sig_odd = spec[:HALF], spec[HALF:]
     joint = jnp.concatenate(
         [sig_even * even - sig_odd * cross, sig_even * cross + sig_odd * last], axis=0
     )
     joint_hi = joint.astype(jnp.bfloat16)
-    joint_lo = (joint - joint_hi.astype(jnp.float32)).astype(jnp.bfloat16)
+    return joint_hi, (joint - joint_hi.astype(jnp.float32)).astype(jnp.bfloat16)
+
+
+def backward_part(bwd, joint_hi, joint_lo):
     back = dot32(bwd, joint_hi)
-    filtered = back[:HALF] + back[HALF:] + dot32(bwd[:HALF], joint_lo)
+    return back[:HALF] + back[HALF:] + dot32(bwd[:HALF], joint_lo)
+
+
+def gated(filtered, here, skip, query, resid):
     mixed = filtered + skip * here.astype(jnp.float32)
     return (resid.astype(jnp.float32) + query.astype(jnp.float32) * mixed).astype(jnp.bfloat16)
+
+
+def filtered_result(spec, taps, here, skip, query, resid, bwd):
+    return gated(backward_part(bwd, *joint_parts(spec, taps)), here, skip, query, resid)
 
 
 def squares_added(total, result):
@@ -239,27 +249,34 @@
 ):
     rows = pl.ds(0, HALF)
     total = None
-    spec = None
     starts = list(range(0, here_ref.shape[1], WIDE))
-    for index in range(len(starts) + 1):
-        ready = spec
-        if index < len(starts):
-            cols = pl.ds(starts[index], WIDE)
-            signal = jnp.concatenate([before_ref[:, cols], here_ref[:, cols]], axis=0)
-            spec = forward_part(fwd_ref[...], signal)
-        if index > 0:
-            cols = pl.ds(starts[index - 1], WIDE)
-            result = filtered_result(
-                ready,
-                (even_ref[:, cols], cross_ref[:, cols], last_ref[:, cols]),
+    specs, joints, backs = {}, {}, {}
+    for index in range(len(starts) + 3):
+        chunk = index - 3
+        if chunk >= 0:
+            cols = pl.ds(starts[chunk], WIDE)
+            result = gated(
+                backs.pop(chunk),
                 here_ref[:, cols],
                 skip_ref[:, cols],
                 query_ref[rows, cols],
                 resid_ref[rows, cols],
-                bwd_ref[...],
             )
             out_ref[:, cols] = result
             total = squares_added(total, result)
+        chunk = index - 2
+        if 0 <= chunk < len(starts):
+            backs[chunk] = backward_part(bwd_ref[...], *joints.pop(chunk))
+        chunk = index
+        if chunk < len(starts):
+            cols = pl.ds(starts[chunk], WIDE)
+            signal = jnp.concatenate([before_ref[:, cols], here_ref[:, cols]], axis=0)
+            specs[chunk] = forward_part(fwd_ref[...], signal)
+        chunk = index - 1
+        if 0 <= chunk < len(starts):
+            cols = pl.ds(starts[chunk], WIDE)
+            taps = (even_ref[:, cols], cross_ref[:, cols], last_ref[:, cols])
+            joints[chunk] = joint_parts(specs.pop(chunk), taps)
     write_squares(total, square_ref)
 
 
@@ -303,13 +320,41 @@
     return held
 
 
+def ready_kernel(part_ref, key_ref, gain_ref, rate_ref, scaled_ref, reach_ref):
+    remaining = (sublane_iota() - (SUB - 1)).astype(jnp.float32) * float(STEPS)
+
+    def body(block, cols, side):
+        scaled_ref[:, cols] = (
+            key_ref[:HALF, cols].astype(jnp.float32)
+            * part_ref[:, cols].astype(jnp.float32)
+            * gain_ref[:, cols]
+        )
+        for m in range(rate_ref.shape[0]):
+            reach_ref[block, m] = jnp.exp(row_of(rate_ref, m, cols) * remaining)
+
+    lane_blocks(rate_ref.shape[1], body)
+
+
+def made_ready(part, key, gain, rates):
+    modes, channels = rates.shape
+    return local_call(
+        ready_kernel,
+        "ready",
+        [
+            shape_of(part.shape, jnp.float32),
+            shape_of((channels // LANES, modes, SUB, LANES), jnp.float32),
+        ],
+        (part, key, gain, rates),
+    )
+
+
 def state_kernel(row_start, total_channels, last, *refs):
-    part_ref, key_ref, near_ref, far_ref, gain_ref, rate_ref = refs[:6]
     if last:
-        later_ref = refs[6]
+        part_ref, near_ref, far_ref, rate_ref, scaled_ref, reach_ref, later_ref = refs[:7]
         value_ref, state_ref, joined_ref, wide_ref, scale_ref, decay_ref, sems = refs[8:]
         made_ref = value_ref
     else:
+        part_ref, near_ref, far_ref, rate_ref, key_ref, gain_ref = refs[:6]
         value_ref, state_ref, joined_ref, end_ref = refs[6:10]
         wide_ref, scale_ref, decay_ref, sems, made_ref, held_ref = refs[10:]
     join = pltpu.make_async_copy(
@@ -323,12 +368,15 @@
 
     def body(block, cols, side):
         decay_ref[side] = jnp.exp(-rate_ref[:, cols])
-        value = (
-            key_ref[rows, cols].astype(jnp.float32)
-            * part_ref[:, cols].astype(jnp.float32)
-            * scale_ref[...]
-            * gain_ref[:, cols]
-        ).astype(jnp.bfloat16)
+        if last:
+            scaled = scaled_ref[:, cols]
+        else:
+            scaled = (
+                key_ref[rows, cols].astype(jnp.float32)
+                * part_ref[:, cols].astype(jnp.float32)
+                * gain_ref[:, cols]
+            )
+        value = (scaled * scale_ref[...]).astype(jnp.bfloat16)
         made_ref[:, cols] = value
         wide_ref[side] = value.astype(jnp.float32)
         held = swept(wide_ref.at[side], decay_ref.at[side])
@@ -341,9 +389,11 @@
         tiles = []
         for group in range(modes // SUB):
             span = range(group * SUB, (group + 1) * SUB)
-            state = gathered_sums(
-                [held[m] * jnp.exp(row_of(rate_ref, m, cols) * remaining) for m in span]
-            )
+            if last:
+                reach = [reach_ref[block, m] for m in span]
+            else:
+                reach = [jnp.exp(row_of(rate_ref, m, cols) * remaining) for m in span]
+            state = gathered_sums([held[m] * r for m, r in zip(span, reach)])
             if last:
                 rate = rate_ref[group * SUB : (group + 1) * SUB, cols]
                 state = later_ref[group, block] + jnp.exp(-rate * float(HALF)) * state
@@ -376,7 +426,7 @@
     return values[0]
 
 
-def half_states(part, key, near, far, gain, rates, row_start, total_channels, last=()):
+def half_states(part, near, far, rates, extra, row_start, total_channels, last=()):
     channels = part.shape[1]
     modes = rates.shape[0]
     blocks = channels // LANES
@@ -401,7 +451,7 @@
         functools.partial(state_kernel, row_start, total_channels, len(last)),
         "states",
         outputs,
-        (part, key, near, far, gain, rates, *last),
+        (part, near, far, rates, *extra, *last),
         scratch,
         far_in=(7,) if last else (),
         far_out=(2,) if last else (0, 2, 3),
@@ -734,21 +784,22 @@
     far_high = across_pairs(near_high)
     total_channels = channels * lax.axis_size("tp")
     value_high, state_high, residual_out, end_high = half_states(
-        high, key_two, near_high, far_high, gain_row, decay_rates, HALF, total_channels
+        high, near_high, far_high, decay_rates, (key_two, gain_row), HALF, total_channels
     )
     before, state_high = lax.optimization_barrier((before, state_high))
     low, square_low = lower_block(
         before, product_low, spectrum, query_one, residual_in, skip_row, tables
     )
     near_low = summed_with_pair(square_low)
+    near_low, low = lax.optimization_barrier((near_low, low))
     far_low = across_pairs(near_low)
+    ready = made_ready(low, key_two, gain_row, decay_rates)
     value_low, state, residual_out = half_states(
         low,
-        key_two,
         near_low,
         far_low,
-        gain_row,
         decay_rates,
+        ready,
         0,
         total_channels,
         (state_high, residual_out),

time: 63.8 us -> 63.3 us (level)
    pallas_call x7 -> x8, Pallas kernels: 23.6 us -> 23.7 us  [local_call(): call(*[pltpu.with_memory_space_constraint(operand, HBM if k in far_in els...]
  transfers between devices with their start and end apart: 6 -> 6, of which waited for: 5 -> 5; matrix products, arithmetic and copies ran while one was open for 0% -> 0% of each run, Pallas kernels for 21% -> 22%
where the time goes in v3:
time: 63.3 us; the launch traced here: 63 us
  Pallas kernels  23.7 us (37%)
  starting transfers between devices  18.5 us (29%)
  blocking collectives  10.8 us (17%)
  waiting for transfers between devices  7.93 us (13%)
  other arithmetic  1.26 us (2%)
  between operations  0.84 us (1%)
    pallas_call x8, Pallas kernels, local_call(): call(*[pltpu.with_memory_space_constraint(operand, HBM if k in far_in els...  23.7 us
    all_to_all x1, blocking collectives, on_device(): lax.all_to_all(total, 'ctx', split_axis=0, concat_axis=0, tiled=True, axi...  10.8 us
    all_to_all x1, starting transfers between devices, on_device(): lax.all_to_all(state, 'ctx', split_axis=0, concat_axis=0, tiled=True, axi...  8.29 us
    ppermute x2, starting transfers between devices, across_pairs(): return lax.ppermute(value, 'tp', [(0, 2), (2, 0), (1, 3), (3, 1)])  6.04 us
    ppermute x1, starting transfers between devices, on_device(): lax.ppermute(product_high, 'ctx', [(d, d + 1) for d in range(count - 1)])  3.97 us
    ppermute x2, waiting for transfers between devices, across_pairs(): return lax.ppermute(value, 'tp', [(0, 2), (2, 0), (1, 3), (3, 1)])  3.68 us
    ppermute x2, waiting for transfers between devices, summed_with_pair(): return value + lax.ppermute(value, 'tp', [(0, 1), (1, 0), (2, 3), (3, 2)])  2.31 us
    all_to_all x1, waiting for transfers between devices, on_device(): lax.all_to_all(state, 'ctx', split_axis=0, concat_axis=0, tiled=True, axi...  1.94 us
  transfers between devices with their start and end apart: 6, of which 5 were waited for; matrix products, arithmetic and copies ran while one was open for 0% of the time, Pallas kernels for 22%

profile of v3, /device:TPU:0, one launch (start us, length us, event | category | flops | bytes accessed | tf_op | source)
XLA Modules:
  0.0 63.0 jit_solution(11597623592297838267)
XLA Ops:
  0.6 1.3 %slice_multiply_fusion.here_ref = bf16[128,2048]{1,0:T(8,128)(2,1)S(1)} fusion(bf16[256,2048]{1,0:T(8,128)(2,1)} %value_far.1, bf16[256,2048]{1,0:T(8,128)(2,1)} %key_far.1), kind=kLoop, calls=%fused_computation | loop fusion | flops 262144 | bytes 1572864 | tf_op jit(solution)/shard_map/mul | solution.py:777
  1.9 4.0 %collective-permute-start = (bf16[128,2048]{1,0:T(8,128)(2,1)S(1)}, bf16[128,2048]{1,0:T(8,128)(2,1)S(1)}, u32[]{:S(2)}, u32[]{:S(2)}) collective-permute-start(bf16[128,2048]{1,0:T(8,128)(2,1)S(1)} %slice_multiply_fusion.here_ref), channel_id=1, source_target_pairs={{0,4},{4,8},{8,12},{12,16},{16,20},{20,24},{24,28},{28,32},{32,36}... | collective-permute-start | bytes 1572872 | tf_op jit(solution)/shard_map/ppermute | solution.py:779
  5.9 0.0 copy-start
  5.9 0.0 copy-start.3
  5.9 0.0 copy-start.8
  5.9 0.0 copy-start.2
  5.9 0.0 copy-start.4
  5.9 0.0 copy-start.6
  5.9 0.0 copy-start.7
  5.9 3.9 %upper.1 = (bf16[128,2048]{1,0:T(8,128)(2,1)S(1)}, f32[8,128]{1,0:T(8,128)S(1)}, bf16[128,2048]{1,0:T(8,128)(2,1)S(1)}, f32[128,2048]{1,0:T(8,128)S(1)}, f32[128...) custom-call(bf16[128,2048]{1,0:T(8,128)(2,1)S(1)} %slice_multiply_fusion.here_ref, bf16[256,2048]{1,0:T(8,128)(2,1)} %key_far.1, ...), custom_call_target="tpu_custom_call" | custom-call | tf_op jit(solution)/shard_map/upper/pallas_call | solution.py:66
  9.8 0.0 copy-start.1
  9.8 0.1 collective-permute-start.1
  9.9 1.2 %collective-permute-done.1 = f32[8,128]{1,0:T(8,128)S(1)} collective-permute-done((f32[8,128]{1,0:T(8,128)S(1)}, f32[8,128]{1,0:T(8,128)S(1)}, u32[]{:S(2)}, u32[]{:S(2)}) %collective-permute-start.1) | collective-permute-done | bytes 4128 | tf_op jit(solution)/shard_map/ppermute | solution.py:747
  11.1 3.0 %collective-permute-start.2 = (f32[8,128]{1,0:T(8,128)S(1)}, f32[8,128]{1,0:T(8,128)S(1)}, u32[]{:S(2)}, u32[]{:S(2)}) collective-permute-start(f32[8,128]{1,0:T(8,128)S(1)} %add.6.refs_1_), channel_id=1, source_target_pairs={{0,2},{2,0},{1,3},{3,1},{4,6},{6,4},{5,7},{7,5},{8,10},{10,8},{9,1... | collective-permute-start | bytes 12296 | tf_op jit(solution)/shard_map/ppermute | solution.py:751
  14.1 2.1 %collective-permute-done.2.refs_2_ = f32[8,128]{1,0:T(8,128)S(1)} collective-permute-done((f32[8,128]{1,0:T(8,128)S(1)}, f32[8,128]{1,0:T(8,128)S(1)}, u32[]{:S(2)}, u32[]{:S(2)}) %collective-permute-start.2) | collective-permute-done | bytes 4128 | tf_op jit(solution)/shard_map/ppermute | solution.py:751
  16.2 0.0 copy-done
  16.2 0.0 copy-done.3
  16.2 0.0 copy-done.8
  16.2 2.8 %states.2 = (bf16[128,2048]{1,0:T(8,128)(2,1)}, f32[2,16,8,128]{3,2,1,0:T(8,128)S(1)}, bf16[256,2048]{1,0:T(8,128)(2,1)}, f32[16,16,8,128]{3,2,1,0:T(8,128)}) custom-call(bf16[128,2048]{1,0:T(8,128)(2,1)S(1)} %get-tuple-element.30.refs_0_, f32[8,128]{1,0:T(8,128)S(1)} %add.6.refs_1_, f32[8,128]{1,0:T(8,128)S(1)} %collective-permute-done.2.refs_2_, ...), custom_call_target="tpu_custom_call" | custom-call | tf_op jit(solution)/shard_map/states/pallas_call | solution.py:66
  19.0 0.0 collective-permute-done.before_ref
  19.1 0.0 copy-done.2
  19.1 0.0 copy-done.4
  19.1 0.0 copy-done.6
  19.1 0.0 copy-done.7
  19.1 0.0 copy-done.1
  19.1 2.0 %lower.1 = (bf16[128,2048]{1,0:T(8,128)(2,1)S(1)}, f32[8,128]{1,0:T(8,128)S(1)}) custom-call(bf16[128,2048]{1,0:T(8,128)(2,1)S(1)} %collective-permute-done.before_ref, bf16[128,2048]{1,0:T(8,128)(2,1)S(1)} %get-tuple-element.34.here_ref, f32[128,2048]{1,0:T(8,128)S(1)} %get-tuple-element.35.even_ref, f32[128,2048]{1,0:T(8,128)S(1)} %get-tuple-element.36.cross_ref, ...), custom_call_target="tpu_custom_call" | custom-call | tf_op jit(solution)/shard_map/lower/pallas_call | solution.py:66
  21.1 0.1 collective-permute-start.3
  21.2 1.2 %collective-permute-done.3 = f32[8,128]{1,0:T(8,128)S(1)} collective-permute-done((f32[8,128]{1,0:T(8,128)S(1)}, f32[8,128]{1,0:T(8,128)S(1)}, u32[]{:S(2)}, u32[]{:S(2)}) %collective-permute-start.3) | collective-permute-done | bytes 4128 | tf_op jit(solution)/shard_map/ppermute | solution.py:747
  22.3 3.0 %collective-permute-start.4 = (f32[8,128]{1,0:T(8,128)S(1)}, f32[8,128]{1,0:T(8,128)S(1)}, u32[]{:S(2)}, u32[]{:S(2)}) collective-permute-start(f32[8,128]{1,0:T(8,128)S(1)} %add.7.refs_1_), channel_id=1, source_target_pairs={{0,2},{2,0},{1,3},{3,1},{4,6},{6,4},{5,7},{7,5},{8,10},{10,8},{9,1... | collective-permute-start | bytes 12296 | tf_op jit(solution)/shard_map/ppermute | solution.py:751
  25.3 0.5 ready.1
  25.8 1.6 %collective-permute-done.4.refs_2_ = f32[8,128]{1,0:T(8,128)S(1)} collective-permute-done((f32[8,128]{1,0:T(8,128)S(1)}, f32[8,128]{1,0:T(8,128)S(1)}, u32[]{:S(2)}, u32[]{:S(2)}) %collective-permute-start.4) | collective-permute-done | bytes 4128 | tf_op jit(solution)/shard_map/ppermute | solution.py:751
  27.4 0.0 copy-start.5
  27.4 0.0 copy-start.9
  27.4 2.6 %states.3 = (bf16[128,2048]{1,0:T(8,128)(2,1)S(1)}, bf16[8,16,2048]{2,1,0:T(8,128)(2,1)}, bf16[256,2048]{1,0:T(8,128)(2,1)}) custom-call(bf16[128,2048]{1,0:T(8,128)(2,1)S(1)} %get-tuple-element.40.part_ref.refs_0_, f32[8,128]{1,0:T(8,128)S(1)} %add.7.refs_1_, f32[8,128]{1,0:T(8,128)S(1)} %collective-permute-done.4.refs_2_, ...), custom_call_target="tpu_custom_call", output_to_operand_aliasing={{2}: (7, {})} | custom-call | tf_op jit(solution)/shard_map/states/pallas_call | solution.py:66
  30.1 8.3 %all-to-all-start = ((bf16[8,16,2048]{2,1,0:T(8,128)(2,1)}), bf16[8,16,2048]{2,1,0:T(8,128)(2,1)S(1)}, u32[]{:S(2)}, u32[]{:S(2)}) async-start(bf16[8,16,2048]{2,1,0:T(8,128)(2,1)} %get-tuple-element.47), calls=%async_computation | async-start | bytes 1048576 | tf_op jit(solution)/shard_map/all_to_all | solution.py:810
  38.4 0.0 copy-done.5
  38.4 0.0 copy-done.9
  38.4 6.9 %inner.1 = (f32[16,256,128]{2,1,0:T(8,128)}, f32[16,2,16,8,128]{4,3,2,1,0:T(8,128)S(1)}) custom-call(bf16[128,2048]{1,0:T(8,128)(2,1)S(1)} %get-tuple-element.48.low_ref, bf16[128,2048]{1,0:T(8,128)(2,1)} %get-tuple-element.49.far_value_ref, f32[16,16,8,128]{3,2,1,0:T(8,128)} %get-tuple-element.50.far_end_ref, f32[16,2048]{1,0:T(8,128)S(1)} %copy-done, ...), custom_call_target="tpu_custom_call" | custom-call | tf_op jit(solution)/shard_map/inner/pallas_call | solution.py:66
  45.3 1.9 %all-to-all-done.state_ref = bf16[8,16,2048]{2,1,0:T(8,128)(2,1)S(1)} async-done(((bf16[8,16,2048]{2,1,0:T(8,128)(2,1)}), bf16[8,16,2048]{2,1,0:T(8,128)(2,1)S(1)}, u32[]{:S(2)}, u32[]{:S(2)}) %all-to-all-start) | async-done | bytes 524320 | tf_op jit(solution)/shard_map/all_to_all | solution.py:810
  47.2 0.3 group.1
  47.5 10.8 %all_to_all.10.totals_ref = bf16[4,16,2048]{2,1,0:T(8,128)(2,1)S(1)} all-to-all(bf16[4,16,2048]{2,1,0:T(8,128)(2,1)S(1)} %get-tuple-element.57), channel_id=1, replica_groups={{0,32,64,96},{4,36,68,100},{8,40,72,104},{12,44,76,108},{16,48,80,112},..., dimensions={0} | all-to-all | bytes 524288 | tf_op jit(solution)/shard_map/all_to_all | solution.py:819
  58.3 4.7 %output.1 = bf16[256,2048]{1,0:T(8,128)(2,1)} custom-call(f32[16,256,128]{2,1,0:T(8,128)} %get-tuple-element.53.near_ref, f32[16,2,16,8,128]{4,3,2,1,0:T(8,128)S(1)} %get-tuple-element.54.prefix_ref, f32[16,2048]{1,0:T(8,128)S(1)} %get-tuple-element.56.before_ref, bf16[4,16,2048]{2,1,0:T(8,128)(2,1)S(1)} %all_to_all.10.totals_ref, f32[16,2048]{1,0:T(8,128)S(1)} %copy-done, ...), custom_call_target="tpu_custom_call" | custom-call | tf_op jit(solution)/shard_map/output/pallas_call | solution.py:66
  (2 shorter events, 0.0 us)
Async XLA Ops:
  1.9 17.2 %collective-permute-start = (bf16[128,2048]{1,0:T(8,128)(2,1)S(1)}, bf16[128,2048]{1,0:T(8,128)(2,1)S(1)}, u32[]{:S(2)}, u32[]{:S(2)}) collective-permute-start(bf16[128,2048]{1,0:T(8,128)(2,1)S(1)} %slice_multiply_fusion.here_ref), channel_id=1, source_target_pairs={{0,4},{4,8},{8,12},{12,16},{16,20},{20,24},{24,28},{28,32},{32,36}... | collective-permute-start | bytes 1572872 | tf_op jit(solution)/shard_map/ppermute | solution.py:779
  5.9 10.3 %copy-start = (f32[16,2048]{1,0:T(8,128)S(1)}, f32[16,2048]{1,0:T(8,128)}, u32[]{:S(2)}) copy-start(f32[16,2048]{1,0:T(8,128)} %rate_ref.7) | copy-start | bytes 393220
  5.9 10.3 %copy-start.3 = (bf16[256,2048]{1,0:T(8,128)(2,1)S(1)}, bf16[256,2048]{1,0:T(8,128)(2,1)}, u32[]{:S(2)}) copy-start(bf16[256,2048]{1,0:T(8,128)(2,1)} %key_ref.1) | copy-start | bytes 3145732
  5.9 10.3 %copy-start.8 = (f32[2048]{0:T(1024)S(1)}, f32[2048]{0:T(1024)}, u32[]{:S(2)}) copy-start(f32[2048]{0:T(1024)} %param.20) | copy-start | bytes 24580
  5.9 13.2 %copy-start.2 = (bf16[256,2048]{1,0:T(8,128)(2,1)S(1)}, bf16[256,2048]{1,0:T(8,128)(2,1)}, u32[]{:S(2)}) copy-start(bf16[256,2048]{1,0:T(8,128)(2,1)} %resid_ref.1) | copy-start | bytes 3145732
  5.9 13.2 %copy-start.4 = (bf16[512,256]{1,0:T(8,128)(2,1)S(1)}, bf16[512,256]{1,0:T(8,128)(2,1)}, u32[]{:S(2)}) copy-start(bf16[512,256]{1,0:T(8,128)(2,1)} %constant.4.clone.fwd_far.fwd_ref) | copy-start | bytes 786436
  5.9 13.2 %copy-start.6 = (bf16[256,256]{1,0:T(8,128)(2,1)S(1)}, bf16[256,256]{1,0:T(8,128)(2,1)}, u32[]{:S(2)}) copy-start(bf16[256,256]{1,0:T(8,128)(2,1)} %constant.5.clone.bwd_far.bwd_ref) | copy-start | bytes 393220
  5.9 13.1 %copy-start.7 = (f32[2048]{0:T(1024)S(1)}, f32[2048]{0:T(1024)}, u32[]{:S(2)}) copy-start(f32[2048]{0:T(1024)} %param.19) | copy-start | bytes 24580
  9.8 9.3 %copy-start.1 = (bf16[256,2048]{1,0:T(8,128)(2,1)S(1)}, bf16[256,2048]{1,0:T(8,128)(2,1)}, u32[]{:S(2)}) copy-start(bf16[256,2048]{1,0:T(8,128)(2,1)} %query_ref.2) | copy-start | bytes 3145732
  9.8 1.2 %collective-permute-start.1 = (f32[8,128]{1,0:T(8,128)S(1)}, f32[8,128]{1,0:T(8,128)S(1)}, u32[]{:S(2)}, u32[]{:S(2)}) collective-permute-start(f32[8,128]{1,0:T(8,128)S(1)} %get-tuple-element.31), channel_id=1, source_target_pairs={{0,1},{1,0},{2,3},{3,2},{4,5},{5,4},{6,7},{7,6},{8,9},{9,8},{10,11... | collective-permute-start | bytes 12296 | tf_op jit(solution)/shard_map/ppermute | solution.py:747
  11.1 5.1 %collective-permute-start.2 = (f32[8,128]{1,0:T(8,128)S(1)}, f32[8,128]{1,0:T(8,128)S(1)}, u32[]{:S(2)}, u32[]{:S(2)}) collective-permute-start(f32[8,128]{1,0:T(8,128)S(1)} %add.6.refs_1_), channel_id=1, source_target_pairs={{0,2},{2,0},{1,3},{3,1},{4,6},{6,4},{5,7},{7,5},{8,10},{10,8},{9,1... | collective-permute-start | bytes 12296 | tf_op jit(solution)/shard_map/ppermute | solution.py:751
  21.1 1.2 %collective-permute-start.3 = (f32[8,128]{1,0:T(8,128)S(1)}, f32[8,128]{1,0:T(8,128)S(1)}, u32[]{:S(2)}, u32[]{:S(2)}) collective-permute-start(f32[8,128]{1,0:T(8,128)S(1)} %get-tuple-element.38), channel_id=1, source_target_pairs={{0,1},{1,0},{2,3},{3,2},{4,5},{5,4},{6,7},{7,6},{8,9},{9,8},{10,11... | collective-permute-start | bytes 12296 | tf_op jit(solution)/shard_map/ppermute | solution.py:747
  22.3 5.1 %collective-permute-start.4 = (f32[8,128]{1,0:T(8,128)S(1)}, f32[8,128]{1,0:T(8,128)S(1)}, u32[]{:S(2)}, u32[]{:S(2)}) collective-permute-start(f32[8,128]{1,0:T(8,128)S(1)} %add.7.refs_1_), channel_id=1, source_target_pairs={{0,2},{2,0},{1,3},{3,1},{4,6},{6,4},{5,7},{7,5},{8,10},{10,8},{9,1... | collective-permute-start | bytes 12296 | tf_op jit(solution)/shard_map/ppermute | solution.py:751
  27.4 11.0 %copy-start.5 = (f32[16,2048]{1,0:T(8,128)S(1)}, f32[16,2048]{1,0:T(8,128)}, u32[]{:S(2)}) copy-start(f32[16,2048]{1,0:T(8,128)} %residue_ref.3) | copy-start | bytes 393220
  27.4 11.0 %copy-start.9 = (f32[2048]{0:T(1024)S(1)}, f32[2048]{0:T(1024)}, u32[]{:S(2)}) copy-start(f32[2048]{0:T(1024)} %param.25) | copy-start | bytes 24580
  30.1 17.1 %all-to-all-start = ((bf16[8,16,2048]{2,1,0:T(8,128)(2,1)}), bf16[8,16,2048]{2,1,0:T(8,128)(2,1)S(1)}, u32[]{:S(2)}, u32[]{:S(2)}) async-start(bf16[8,16,2048]{2,1,0:T(8,128)(2,1)} %get-tuple-element.47), calls=%async_computation | async-start | bytes 1048576 | tf_op jit(solution)/shard_map/all_to_all | solution.py:810

commit v4 on v3

--- a/solution.py
+++ b/solution.py
@@ -13,7 +13,7 @@
 LANES = 128
 SUB = 8
 STEPS = HALF // SUB
-WIDE = 256
+WIDE = 512
 GROUP = 8
 
 

time: 63.3 us -> 63 us (level)
  no operation moved by 1% of the time
where the time goes in v4:
time: 63 us; the launch traced here: 62.7 us
  Pallas kernels  23.4 us (37%)
  starting transfers between devices  18.5 us (29%)
  blocking collectives  10.8 us (17%)
  waiting for transfers between devices  7.91 us (13%)
  other arithmetic  1.26 us (2%)
  between operations  0.84 us (1%)
    pallas_call x8, Pallas kernels, local_call(): call(*[pltpu.with_memory_space_constraint(operand, HBM if k in far_in els...  23.4 us
    all_to_all x1, blocking collectives, on_device(): lax.all_to_all(total, 'ctx', split_axis=0, concat_axis=0, tiled=True, axi...  10.8 us
    all_to_all x1, starting transfers between devices, on_device(): lax.all_to_all(state, 'ctx', split_axis=0, concat_axis=0, tiled=True, axi...  8.27 us
    ppermute x2, starting transfers between devices, across_pairs(): return lax.ppermute(value, 'tp', [(0, 2), (2, 0), (1, 3), (3, 1)])  6.06 us
    ppermute x1, starting transfers between devices, on_device(): lax.ppermute(product_high, 'ctx', [(d, d + 1) for d in range(count - 1)])  3.97 us
    ppermute x2, waiting for transfers between devices, across_pairs(): return lax.ppermute(value, 'tp', [(0, 2), (2, 0), (1, 3), (3, 1)])  3.66 us
    ppermute x2, waiting for transfers between devices, summed_with_pair(): return value + lax.ppermute(value, 'tp', [(0, 1), (1, 0), (2, 3), (3, 2)])  2.31 us
    all_to_all x1, waiting for transfers between devices, on_device(): lax.all_to_all(state, 'ctx', split_axis=0, concat_axis=0, tiled=True, axi...  1.94 us
  transfers between devices with their start and end apart: 6, of which 5 were waited for; matrix products, arithmetic and copies ran while one was open for 0% of the time, Pallas kernels for 22%

profile of v4, /device:TPU:0, one launch (start us, length us, event | category | flops | bytes accessed | tf_op | source)
XLA Modules:
  0.0 62.7 jit_solution(18158813992464807117)
XLA Ops:
  0.6 1.3 %slice_multiply_fusion.here_ref = bf16[128,2048]{1,0:T(8,128)(2,1)S(1)} fusion(bf16[256,2048]{1,0:T(8,128)(2,1)} %value_far.1, bf16[256,2048]{1,0:T(8,128)(2,1)} %key_far.1), kind=kLoop, calls=%fused_computation | loop fusion | flops 262144 | bytes 1572864 | tf_op jit(solution)/shard_map/mul | solution.py:777
  1.9 4.0 %collective-permute-start = (bf16[128,2048]{1,0:T(8,128)(2,1)S(1)}, bf16[128,2048]{1,0:T(8,128)(2,1)S(1)}, u32[]{:S(2)}, u32[]{:S(2)}) collective-permute-start(bf16[128,2048]{1,0:T(8,128)(2,1)S(1)} %slice_multiply_fusion.here_ref), channel_id=1, source_target_pairs={{0,4},{4,8},{8,12},{12,16},{16,20},{20,24},{24,28},{28,32},{32,36}... | collective-permute-start | bytes 1572872 | tf_op jit(solution)/shard_map/ppermute | solution.py:779
  5.9 0.0 copy-start
  5.9 0.0 copy-start.3
  5.9 0.0 copy-start.8
  5.9 0.0 copy-start.2
  5.9 0.0 copy-start.4
  5.9 0.0 copy-start.6
  5.9 0.0 copy-start.7
  5.9 3.9 %upper.1 = (bf16[128,2048]{1,0:T(8,128)(2,1)S(1)}, f32[8,128]{1,0:T(8,128)S(1)}, bf16[128,2048]{1,0:T(8,128)(2,1)S(1)}, f32[128,2048]{1,0:T(8,128)S(1)}, f32[128...) custom-call(bf16[128,2048]{1,0:T(8,128)(2,1)S(1)} %slice_multiply_fusion.here_ref, bf16[256,2048]{1,0:T(8,128)(2,1)} %key_far.1, ...), custom_call_target="tpu_custom_call" | custom-call | tf_op jit(solution)/shard_map/upper/pallas_call | solution.py:66
  9.8 0.0 copy-start.1
  9.8 0.1 collective-permute-start.1
  9.9 1.2 %collective-permute-done.1 = f32[8,128]{1,0:T(8,128)S(1)} collective-permute-done((f32[8,128]{1,0:T(8,128)S(1)}, f32[8,128]{1,0:T(8,128)S(1)}, u32[]{:S(2)}, u32[]{:S(2)}) %collective-permute-start.1) | collective-permute-done | bytes 4128 | tf_op jit(solution)/shard_map/ppermute | solution.py:747
  11.1 3.0 %collective-permute-start.2 = (f32[8,128]{1,0:T(8,128)S(1)}, f32[8,128]{1,0:T(8,128)S(1)}, u32[]{:S(2)}, u32[]{:S(2)}) collective-permute-start(f32[8,128]{1,0:T(8,128)S(1)} %add.6.refs_1_), channel_id=1, source_target_pairs={{0,2},{2,0},{1,3},{3,1},{4,6},{6,4},{5,7},{7,5},{8,10},{10,8},{9,1... | collective-permute-start | bytes 12296 | tf_op jit(solution)/shard_map/ppermute | solution.py:751
  14.1 2.1 %collective-permute-done.2.refs_2_ = f32[8,128]{1,0:T(8,128)S(1)} collective-permute-done((f32[8,128]{1,0:T(8,128)S(1)}, f32[8,128]{1,0:T(8,128)S(1)}, u32[]{:S(2)}, u32[]{:S(2)}) %collective-permute-start.2) | collective-permute-done | bytes 4128 | tf_op jit(solution)/shard_map/ppermute | solution.py:751
  16.2 0.0 copy-done
  16.2 0.0 copy-done.3
  16.2 0.0 copy-done.8
  16.2 2.8 %states.2 = (bf16[128,2048]{1,0:T(8,128)(2,1)}, f32[2,16,8,128]{3,2,1,0:T(8,128)S(1)}, bf16[256,2048]{1,0:T(8,128)(2,1)}, f32[16,16,8,128]{3,2,1,0:T(8,128)}) custom-call(bf16[128,2048]{1,0:T(8,128)(2,1)S(1)} %get-tuple-element.30.refs_0_, f32[8,128]{1,0:T(8,128)S(1)} %add.6.refs_1_, f32[8,128]{1,0:T(8,128)S(1)} %collective-permute-done.2.refs_2_, ...), custom_call_target="tpu_custom_call" | custom-call | tf_op jit(solution)/shard_map/states/pallas_call | solution.py:66
  19.1 0.0 collective-permute-done.before_ref
  19.1 0.0 copy-done.2
  19.1 0.0 copy-done.4
  19.1 0.0 copy-done.6
  19.1 0.0 copy-done.7
  19.1 0.0 copy-done.1
  19.1 1.7 %lower.1 = (bf16[128,2048]{1,0:T(8,128)(2,1)S(1)}, f32[8,128]{1,0:T(8,128)S(1)}) custom-call(bf16[128,2048]{1,0:T(8,128)(2,1)S(1)} %collective-permute-done.before_ref, bf16[128,2048]{1,0:T(8,128)(2,1)S(1)} %get-tuple-element.34.here_ref, f32[128,2048]{1,0:T(8,128)S(1)} %get-tuple-element.35.even_ref, f32[128,2048]{1,0:T(8,128)S(1)} %get-tuple-element.36.cross_ref, ...), custom_call_target="tpu_custom_call" | custom-call | tf_op jit(solution)/shard_map/lower/pallas_call | solution.py:66
  20.8 0.1 collective-permute-start.3
  20.9 1.2 %collective-permute-done.3 = f32[8,128]{1,0:T(8,128)S(1)} collective-permute-done((f32[8,128]{1,0:T(8,128)S(1)}, f32[8,128]{1,0:T(8,128)S(1)}, u32[]{:S(2)}, u32[]{:S(2)}) %collective-permute-start.3) | collective-permute-done | bytes 4128 | tf_op jit(solution)/shard_map/ppermute | solution.py:747
  22.1 3.0 %collective-permute-start.4 = (f32[8,128]{1,0:T(8,128)S(1)}, f32[8,128]{1,0:T(8,128)S(1)}, u32[]{:S(2)}, u32[]{:S(2)}) collective-permute-start(f32[8,128]{1,0:T(8,128)S(1)} %add.7.refs_1_), channel_id=1, source_target_pairs={{0,2},{2,0},{1,3},{3,1},{4,6},{6,4},{5,7},{7,5},{8,10},{10,8},{9,1... | collective-permute-start | bytes 12296 | tf_op jit(solution)/shard_map/ppermute | solution.py:751
  25.1 0.5 ready.1
  25.6 1.6 %collective-permute-done.4.refs_2_ = f32[8,128]{1,0:T(8,128)S(1)} collective-permute-done((f32[8,128]{1,0:T(8,128)S(1)}, f32[8,128]{1,0:T(8,128)S(1)}, u32[]{:S(2)}, u32[]{:S(2)}) %collective-permute-start.4) | collective-permute-done | bytes 4128 | tf_op jit(solution)/shard_map/ppermute | solution.py:751
  27.2 0.0 copy-start.5
  27.2 0.0 copy-start.9
  27.2 2.6 %states.3 = (bf16[128,2048]{1,0:T(8,128)(2,1)S(1)}, bf16[8,16,2048]{2,1,0:T(8,128)(2,1)}, bf16[256,2048]{1,0:T(8,128)(2,1)}) custom-call(bf16[128,2048]{1,0:T(8,128)(2,1)S(1)} %get-tuple-element.40.part_ref.refs_0_, f32[8,128]{1,0:T(8,128)S(1)} %add.7.refs_1_, f32[8,128]{1,0:T(8,128)S(1)} %collective-permute-done.4.refs_2_, ...), custom_call_target="tpu_custom_call", output_to_operand_aliasing={{2}: (7, {})} | custom-call | tf_op jit(solution)/shard_map/states/pallas_call | solution.py:66
  29.8 8.3 %all-to-all-start = ((bf16[8,16,2048]{2,1,0:T(8,128)(2,1)}), bf16[8,16,2048]{2,1,0:T(8,128)(2,1)S(1)}, u32[]{:S(2)}, u32[]{:S(2)}) async-start(bf16[8,16,2048]{2,1,0:T(8,128)(2,1)} %get-tuple-element.47), calls=%async_computation | async-start | bytes 1048576 | tf_op jit(solution)/shard_map/all_to_all | solution.py:810
  38.1 0.0 copy-done.5
  38.1 0.0 copy-done.9
  38.1 6.9 %inner.1 = (f32[16,256,128]{2,1,0:T(8,128)}, f32[16,2,16,8,128]{4,3,2,1,0:T(8,128)S(1)}) custom-call(bf16[128,2048]{1,0:T(8,128)(2,1)S(1)} %get-tuple-element.48.low_ref, bf16[128,2048]{1,0:T(8,128)(2,1)} %get-tuple-element.49.far_value_ref, f32[16,16,8,128]{3,2,1,0:T(8,128)} %get-tuple-element.50.far_end_ref, f32[16,2048]{1,0:T(8,128)S(1)} %copy-done, ...), custom_call_target="tpu_custom_call" | custom-call | tf_op jit(solution)/shard_map/inner/pallas_call | solution.py:66
  45.0 1.9 %all-to-all-done.state_ref = bf16[8,16,2048]{2,1,0:T(8,128)(2,1)S(1)} async-done(((bf16[8,16,2048]{2,1,0:T(8,128)(2,1)}), bf16[8,16,2048]{2,1,0:T(8,128)(2,1)S(1)}, u32[]{:S(2)}, u32[]{:S(2)}) %all-to-all-start) | async-done | bytes 524320 | tf_op jit(solution)/shard_map/all_to_all | solution.py:810
  46.9 0.3 group.1
  47.2 10.8 %all_to_all.10.totals_ref = bf16[4,16,2048]{2,1,0:T(8,128)(2,1)S(1)} all-to-all(bf16[4,16,2048]{2,1,0:T(8,128)(2,1)S(1)} %get-tuple-element.57), channel_id=1, replica_groups={{0,32,64,96},{4,36,68,100},{8,40,72,104},{12,44,76,108},{16,48,80,112},..., dimensions={0} | all-to-all | bytes 524288 | tf_op jit(solution)/shard_map/all_to_all | solution.py:819
  58.0 4.7 %output.1 = bf16[256,2048]{1,0:T(8,128)(2,1)} custom-call(f32[16,256,128]{2,1,0:T(8,128)} %get-tuple-element.53.near_ref, f32[16,2,16,8,128]{4,3,2,1,0:T(8,128)S(1)} %get-tuple-element.54.prefix_ref, f32[16,2048]{1,0:T(8,128)S(1)} %get-tuple-element.56.before_ref, bf16[4,16,2048]{2,1,0:T(8,128)(2,1)S(1)} %all_to_all.10.totals_ref, f32[16,2048]{1,0:T(8,128)S(1)} %copy-done, ...), custom_call_target="tpu_custom_call" | custom-call | tf_op jit(solution)/shard_map/output/pallas_call | solution.py:66
  (2 shorter events, 0.0 us)
Async XLA Ops:
  1.9 17.2 %collective-permute-start = (bf16[128,2048]{1,0:T(8,128)(2,1)S(1)}, bf16[128,2048]{1,0:T(8,128)(2,1)S(1)}, u32[]{:S(2)}, u32[]{:S(2)}) collective-permute-start(bf16[128,2048]{1,0:T(8,128)(2,1)S(1)} %slice_multiply_fusion.here_ref), channel_id=1, source_target_pairs={{0,4},{4,8},{8,12},{12,16},{16,20},{20,24},{24,28},{28,32},{32,36}... | collective-permute-start | bytes 1572872 | tf_op jit(solution)/shard_map/ppermute | solution.py:779
  5.9 10.3 %copy-start = (f32[16,2048]{1,0:T(8,128)S(1)}, f32[16,2048]{1,0:T(8,128)}, u32[]{:S(2)}) copy-start(f32[16,2048]{1,0:T(8,128)} %rate_ref.7) | copy-start | bytes 393220
  5.9 10.3 %copy-start.3 = (bf16[256,2048]{1,0:T(8,128)(2,1)S(1)}, bf16[256,2048]{1,0:T(8,128)(2,1)}, u32[]{:S(2)}) copy-start(bf16[256,2048]{1,0:T(8,128)(2,1)} %key_ref.1) | copy-start | bytes 3145732
  5.9 10.3 %copy-start.8 = (f32[2048]{0:T(1024)S(1)}, f32[2048]{0:T(1024)}, u32[]{:S(2)}) copy-start(f32[2048]{0:T(1024)} %param.20) | copy-start | bytes 24580
  5.9 13.2 %copy-start.2 = (bf16[256,2048]{1,0:T(8,128)(2,1)S(1)}, bf16[256,2048]{1,0:T(8,128)(2,1)}, u32[]{:S(2)}) copy-start(bf16[256,2048]{1,0:T(8,128)(2,1)} %resid_ref.1) | copy-start | bytes 3145732
  5.9 13.2 %copy-start.4 = (bf16[512,256]{1,0:T(8,128)(2,1)S(1)}, bf16[512,256]{1,0:T(8,128)(2,1)}, u32[]{:S(2)}) copy-start(bf16[512,256]{1,0:T(8,128)(2,1)} %constant.4.clone.fwd_far.fwd_ref) | copy-start | bytes 786436
  5.9 13.2 %copy-start.6 = (bf16[256,256]{1,0:T(8,128)(2,1)S(1)}, bf16[256,256]{1,0:T(8,128)(2,1)}, u32[]{:S(2)}) copy-start(bf16[256,256]{1,0:T(8,128)(2,1)} %constant.5.clone.bwd_far.bwd_ref) | copy-start | bytes 393220
  5.9 13.2 %copy-start.7 = (f32[2048]{0:T(1024)S(1)}, f32[2048]{0:T(1024)}, u32[]{:S(2)}) copy-start(f32[2048]{0:T(1024)} %param.19) | copy-start | bytes 24580
  9.8 9.3 %copy-start.1 = (bf16[256,2048]{1,0:T(8,128)(2,1)S(1)}, bf16[256,2048]{1,0:T(8,128)(2,1)}, u32[]{:S(2)}) copy-start(bf16[256,2048]{1,0:T(8,128)(2,1)} %query_ref.2) | copy-start | bytes 3145732
  9.8 1.2 %collective-permute-start.1 = (f32[8,128]{1,0:T(8,128)S(1)}, f32[8,128]{1,0:T(8,128)S(1)}, u32[]{:S(2)}, u32[]{:S(2)}) collective-permute-start(f32[8,128]{1,0:T(8,128)S(1)} %get-tuple-element.31), channel_id=1, source_target_pairs={{0,1},{1,0},{2,3},{3,2},{4,5},{5,4},{6,7},{7,6},{8,9},{9,8},{10,11... | collective-permute-start | bytes 12296 | tf_op jit(solution)/shard_map/ppermute | solution.py:747
  11.1 5.1 %collective-permute-start.2 = (f32[8,128]{1,0:T(8,128)S(1)}, f32[8,128]{1,0:T(8,128)S(1)}, u32[]{:S(2)}, u32[]{:S(2)}) collective-permute-start(f32[8,128]{1,0:T(8,128)S(1)} %add.6.refs_1_), channel_id=1, source_target_pairs={{0,2},{2,0},{1,3},{3,1},{4,6},{6,4},{5,7},{7,5},{8,10},{10,8},{9,1... | collective-permute-start | bytes 12296 | tf_op jit(solution)/shard_map/ppermute | solution.py:751
  20.8 1.2 %collective-permute-start.3 = (f32[8,128]{1,0:T(8,128)S(1)}, f32[8,128]{1,0:T(8,128)S(1)}, u32[]{:S(2)}, u32[]{:S(2)}) collective-permute-start(f32[8,128]{1,0:T(8,128)S(1)} %get-tuple-element.38), channel_id=1, source_target_pairs={{0,1},{1,0},{2,3},{3,2},{4,5},{5,4},{6,7},{7,6},{8,9},{9,8},{10,11... | collective-permute-start | bytes 12296 | tf_op jit(solution)/shard_map/ppermute | solution.py:747
  22.1 5.1 %collective-permute-start.4 = (f32[8,128]{1,0:T(8,128)S(1)}, f32[8,128]{1,0:T(8,128)S(1)}, u32[]{:S(2)}, u32[]{:S(2)}) collective-permute-start(f32[8,128]{1,0:T(8,128)S(1)} %add.7.refs_1_), channel_id=1, source_target_pairs={{0,2},{2,0},{1,3},{3,1},{4,6},{6,4},{5,7},{7,5},{8,10},{10,8},{9,1... | collective-permute-start | bytes 12296 | tf_op jit(solution)/shard_map/ppermute | solution.py:751
  27.2 10.9 %copy-start.5 = (f32[16,2048]{1,0:T(8,128)S(1)}, f32[16,2048]{1,0:T(8,128)}, u32[]{:S(2)}) copy-start(f32[16,2048]{1,0:T(8,128)} %residue_ref.3) | copy-start | bytes 393220
  27.2 10.9 %copy-start.9 = (f32[2048]{0:T(1024)S(1)}, f32[2048]{0:T(1024)}, u32[]{:S(2)}) copy-start(f32[2048]{0:T(1024)} %param.25) | copy-start | bytes 24580
  29.8 17.1 %all-to-all-start = ((bf16[8,16,2048]{2,1,0:T(8,128)(2,1)}), bf16[8,16,2048]{2,1,0:T(8,128)(2,1)S(1)}, u32[]{:S(2)}, u32[]{:S(2)}) async-start(bf16[8,16,2048]{2,1,0:T(8,128)(2,1)} %get-tuple-element.47), calls=%async_computation | async-start | bytes 1048576 | tf_op jit(solution)/shard_map/all_to_all | solution.py:810
